TPU v7x, 256 devices: a whole 4x4x8 slice. The times are simulated.
256 devices in a mesh: orb: 32 (over x_hi, z, core), gz: 8 (over x_lo, y).
Axes of the slice: x: 4 (x_hi: 2, x_lo: 2; x = x_hi * 2 + x_lo), y: 4, z: 8, core: 2. Of those that a mesh axis runs over, the one named last changes fastest.
Arguments:
- orbitals: bfloat16 [4096, 32, 16, 128], P('orb', 'gz'), may hold values from -6 to 6
- dielectric: float32 [32, 16, 128], P('gz'), may hold values from 1 to 80
- pairs: int32 [32, 2, 16, 2], P('orb'), may hold values from 0 to 127, as said below
- pair_count: int32 [32, 2], P('orb'), may hold values from 4 to 16, as said below
Outputs:
- exchange: float32 [4096, 32, 16, 128], P('orb', 'gz')
Inputs may be any that keep to these rules, and one draw needn't show every extreme that they name: `pairs`: column 0 is an orbital's index within group g, column 1 within the visiting group (g - s) mod 32; slots at or beyond the block's live count hold valid indices too. Live pairs of a block; they fill slots 0 to pair_count - 1.
All inputs are finite; a program needn't handle non-finite values.
Results may differ from a plain program's by a relative error of at most 0.00055.
Values may be sent and summed in bfloat16 or wider, within the bound.
A program may use at most 128 MiB of HBM per device.

v0:
```python
import math

import jax
import jax.numpy as jnp
from jax import lax
from jax.sharding import PartitionSpec as P

PBLK = 8
SWEEPS = 6
STEPS = 2


near_weight = 1.0
far_weight = 0.25
screening = 0.02
coupling = 4.0 * math.pi
offsets = (-2, -1, 1, 2)


def with_halo(x, sides, width):
    for axis, dim in sides:
        peers, length = (lax.axis_size(axis), x.shape[dim])
        up = [(i, (i + 1) % peers) for i in range(peers - 1)]
        down = [(j, i) for i, j in up]
        last = lax.slice_in_dim(x, length - width, length, axis=dim)
        leading = lax.slice_in_dim(x, 0, width, axis=dim)
        before = lax.ppermute(last, axis, up)
        after = lax.ppermute(leading, axis, down)
        x = jnp.concatenate([before, x, after], axis=dim)
    return x


def shifted_2(block, axis, distance):
    devices = range(lax.axis_size(axis))
    route = [((i - distance) % len(devices), i) for i in devices]
    return lax.ppermute(block, axis, route)


def shifted(source, axis_number, offset):
    length = source.shape[axis_number]
    widths = [(0, 0)] * source.ndim
    widths[axis_number] = (2, 2)
    padded = jnp.pad(source, widths)
    return lax.slice_in_dim(padded, 2 + offset, 2 + offset + length, axis=axis_number)


def per_device(orbitals, dielectric, pairs, pair_count):
    planes = orbitals.shape[1]
    slot_total = pairs.shape[2]
    dielectric_rim = with_halo(dielectric, (("gz", 0),), 2)
    center = dielectric_rim[2 : 2 + planes]
    faces = []
    diagonal = screening * center
    for axis_number in range(3):
        for offset in offsets:
            weight = near_weight if abs(offset) == 1 else far_weight
            if axis_number == 0:
                beyond = dielectric_rim[2 + offset : 2 + offset + planes]
            else:
                beyond = shifted(center, axis_number, offset)
            face_weight = weight * 0.5 * (center + beyond)
            faces.append((axis_number, offset, face_weight))
            diagonal = diagonal + face_weight

    def relax(density):
        potential = jnp.zeros(density.shape, jnp.float32)
        for sweep_index in range(SWEEPS):
            padded = with_halo(potential.astype(jnp.bfloat16), (("gz", 1),), 2).astype(
                potential.dtype
            )
            summed = coupling * density
            for axis_number, offset, face_weight in faces:
                if axis_number == 0:
                    neighbor = padded[:, 2 + offset : 2 + offset + planes]
                else:
                    neighbor = shifted(potential, axis_number + 1, offset)
                summed = summed + face_weight * neighbor
            potential = summed / diagonal
        return potential

    slot_ids = jnp.arange(PBLK, dtype=jnp.int32)
    exchange = jnp.zeros(orbitals.shape, jnp.float32)
    for cycle_step in range(1, STEPS + 1):
        visiting = shifted_2(orbitals, "orb", cycle_step)
        chosen = pairs[0, cycle_step - 1]
        live_count = pair_count[0, cycle_step - 1]
        blocks = slot_total // PBLK

        def one_block(number, totals):
            own_part, visit_part = totals
            first_slot = number * PBLK
            chosen_block = lax.dynamic_slice_in_dim(chosen, first_slot, PBLK, 0)
            live_mask = (first_slot + slot_ids < live_count).astype(jnp.float32)
            first_rows = chosen_block[:, 0]
            first_values = orbitals[first_rows].astype(jnp.float32)
            second_values = visiting[chosen_block[:, 1]].astype(jnp.float32)
            potential = relax(first_values * second_values) * live_mask[:, None, None, None]
            own_part = own_part.at[first_rows].add(potential * second_values)
            visit_part = visit_part.at[chosen_block[:, 1]].add(potential * first_values)
            return (own_part, visit_part)

        zeroed = jnp.zeros(orbitals.shape, jnp.float32)
        visit_zero = jnp.zeros(visiting.shape, jnp.float32)
        own_part, visit_part = lax.fori_loop(0, blocks, one_block, (zeroed, visit_zero))
        exchange = exchange + own_part + shifted_2(visit_part, "orb", -cycle_step)
    return exchange


def solution(mesh):
    placed = (
        P("orb", "gz", None, None),
        P("gz", None, None),
        P("orb", None, None, None),
        P("orb", None),
    )
    return jax.shard_map(
        per_device,
        mesh=mesh,
        in_specs=placed,
        out_specs=P("orb", "gz", None, None),
        check_vma=False,
    )
```

profile of v0, /device:TPU:2, one launch (start us, length us, event | category | flops | bytes accessed | tf_op | source)
XLA Modules:
  0.0 494.0 jit_solution(12973893891595644693)
XLA Ops:
  2.7 4.9 collective-permute-start.26
  11.6 65.4 %collective-permute-done.25 = f32[2,16,128]{2,1,0:T(8,128)S(1)} collective-permute-done((f32[2,16,128]{2,1,0:T(8,128)S(1)}, f32[2,16,128]{2,1,0:T(8,128)S(1)}, u32[]{:S(2)}, u32[]{:S(2)}) %collective-permute-start.25) | collective-permute-done | bytes 16416 | tf_op jit(solution)/shard_map/ppermute | solution.py:27
  84.4 146.0 %while.36 = (s32[]{:T(128)}, f32[128,4,16,128]{3,2,1,0:T(8,128)}, f32[128,4,16,128]{3,2,1,0:T(8,128)}, s32[16,2]{0,1:T(2,128)S(1)}, bf16[128,4,16,128]{3,2,1,0:T...) while((s32[]{:T(128)}, f32[128,4,16,128]{3,2,1,0:T(8,128)}, ...), condition=%wide.region_3.4_spmd.clone, body=%wide.region_0.3_spmd.clone.sunk | while | flops 14485582 | bytes 26617152 | solution.py:104
  86.3 6.0 %collective-permute-start = (bf16[8,2,16,128]{3,2,1,0:T(8,128)(2,1)S(1)}, bf16[8,2,16,128]{3,2,1,0:T(8,128)(2,1)S(1)}, u32[]{:S(2)}, u32[]{:S(2)}) collective-permute-start(bf16[8,2,16,128]{3,2,1,0:T(8,128)(2,1)S(1)} %broadcast.402), channel_id=1, source_target_pairs={{1,0},{2,1},{3,2},{4,3},{5,4},{6,5},{7,6},{9,8},{10,9},{11,10},{12... | collective-permute-start | bytes 196616 | tf_op jit(solution)/shard_map/while/body/eval_jaxpr/ppermute | solution.py:28
  103.6 5.8 %collective-permute-done.3 = bf16[8,2,16,128]{3,2,1,0:T(8,128)(2,1)S(1)} collective-permute-done((bf16[8,2,16,128]{3,2,1,0:T(8,128)(2,1)S(1)}, bf16[8,2,16,128]{3,2,1,0:T(8,128)(2,1)S(1)}, u32[]{:S(2)}, u32[]{:S(2)}) %collective-permute-start.3) | collective-permute-done | bytes 65568 | tf_op jit(solution)/shard_map/while/body/eval_jaxpr/ppermute | solution.py:27
  116.1 4.0 collective-permute-done.5
  126.8 4.0 collective-permute-done.7
  137.5 4.0 collective-permute-done.9
  159.2 6.0 %collective-permute-start = (bf16[8,2,16,128]{3,2,1,0:T(8,128)(2,1)S(1)}, bf16[8,2,16,128]{3,2,1,0:T(8,128)(2,1)S(1)}, u32[]{:S(2)}, u32[]{:S(2)}) collective-permute-start(bf16[8,2,16,128]{3,2,1,0:T(8,128)(2,1)S(1)} %broadcast.402), channel_id=1, source_target_pairs={{1,0},{2,1},{3,2},{4,3},{5,4},{6,5},{7,6},{9,8},{10,9},{11,10},{12... | collective-permute-start | bytes 196616 | tf_op jit(solution)/shard_map/while/body/eval_jaxpr/ppermute | solution.py:28
  176.5 6.1 %collective-permute-done.3 = bf16[8,2,16,128]{3,2,1,0:T(8,128)(2,1)S(1)} collective-permute-done((bf16[8,2,16,128]{3,2,1,0:T(8,128)(2,1)S(1)}, bf16[8,2,16,128]{3,2,1,0:T(8,128)(2,1)S(1)}, u32[]{:S(2)}, u32[]{:S(2)}) %collective-permute-start.3) | collective-permute-done | bytes 65568 | tf_op jit(solution)/shard_map/while/body/eval_jaxpr/ppermute | solution.py:27
  189.2 4.0 collective-permute-done.5
  210.6 4.0 collective-permute-done.9
  235.4 146.3 %while.37 = (s32[]{:T(128)}, f32[128,4,16,128]{3,2,1,0:T(8,128)}, f32[128,4,16,128]{3,2,1,0:T(8,128)}, s32[16,2]{0,1:T(2,128)S(1)}, bf16[128,4,16,128]{3,2,1,0:T...) while((s32[]{:T(128)}, f32[128,4,16,128]{3,2,1,0:T(8,128)}, ...), condition=%wide.region_7.8_spmd.clone, body=%wide.region_4.7_spmd.clone.sunk | while | flops 14485582 | bytes 26617152 | solution.py:104
  237.3 6.0 %collective-permute-start.12 = (bf16[8,2,16,128]{3,2,1,0:T(8,128)(2,1)S(1)}, bf16[8,2,16,128]{3,2,1,0:T(8,128)(2,1)S(1)}, u32[]{:S(2)}, u32[]{:S(2)}) collective-permute-start(bf16[8,2,16,128]{3,2,1,0:T(8,128)(2,1)S(1)} %broadcast.410), channel_id=1, source_target_pairs={{1,0},{2,1},{3,2},{4,3},{5,4},{6,5},{7,6},{9,8},{10,9},{11,10},{12... | collective-permute-start | bytes 196616 | tf_op jit(solution)/shard_map/while/body/eval_jaxpr/ppermute | solution.py:28
  246.9 5.3 %collective-permute-start.14 = (bf16[8,2,16,128]{3,2,1,0:T(8,128)(2,1)S(1)}, bf16[8,2,16,128]{3,2,1,0:T(8,128)(2,1)S(1)}, u32[]{:S(2)}, u32[]{:S(2)}) collective-permute-start(bf16[8,2,16,128]{3,2,1,0:T(8,128)(2,1)S(1)} %get-tuple-element.1542), channel_id=1, source_target_pairs={{1,0},{2,1},{3,2},{4,3},{5,4},{6,5},{7,6},{9,8},{10,9},{11,10},{12... | collective-permute-start | bytes 196616 | tf_op jit(solution)/shard_map/while/body/eval_jaxpr/ppermute | solution.py:28
  254.2 6.3 %collective-permute-done.15 = bf16[8,2,16,128]{3,2,1,0:T(8,128)(2,1)S(1)} collective-permute-done((bf16[8,2,16,128]{3,2,1,0:T(8,128)(2,1)S(1)}, bf16[8,2,16,128]{3,2,1,0:T(8,128)(2,1)S(1)}, u32[]{:S(2)}, u32[]{:S(2)}) %collective-permute-start.15) | collective-permute-done | bytes 65568 | tf_op jit(solution)/shard_map/while/body/eval_jaxpr/ppermute | solution.py:27
  288.5 4.0 collective-permute-done.21
  310.2 6.0 %collective-permute-start.12 = (bf16[8,2,16,128]{3,2,1,0:T(8,128)(2,1)S(1)}, bf16[8,2,16,128]{3,2,1,0:T(8,128)(2,1)S(1)}, u32[]{:S(2)}, u32[]{:S(2)}) collective-permute-start(bf16[8,2,16,128]{3,2,1,0:T(8,128)(2,1)S(1)} %broadcast.410), channel_id=1, source_target_pairs={{1,0},{2,1},{3,2},{4,3},{5,4},{6,5},{7,6},{9,8},{10,9},{11,10},{12... | collective-permute-start | bytes 196616 | tf_op jit(solution)/shard_map/while/body/eval_jaxpr/ppermute | solution.py:28
  319.8 5.5 %collective-permute-start.14 = (bf16[8,2,16,128]{3,2,1,0:T(8,128)(2,1)S(1)}, bf16[8,2,16,128]{3,2,1,0:T(8,128)(2,1)S(1)}, u32[]{:S(2)}, u32[]{:S(2)}) collective-permute-start(bf16[8,2,16,128]{3,2,1,0:T(8,128)(2,1)S(1)} %get-tuple-element.1542), channel_id=1, source_target_pairs={{1,0},{2,1},{3,2},{4,3},{5,4},{6,5},{7,6},{9,8},{10,9},{11,10},{12... | collective-permute-start | bytes 196616 | tf_op jit(solution)/shard_map/while/body/eval_jaxpr/ppermute | solution.py:28
  327.7 6.2 %collective-permute-done.15 = bf16[8,2,16,128]{3,2,1,0:T(8,128)(2,1)S(1)} collective-permute-done((bf16[8,2,16,128]{3,2,1,0:T(8,128)(2,1)S(1)}, bf16[8,2,16,128]{3,2,1,0:T(8,128)(2,1)S(1)}, u32[]{:S(2)}, u32[]{:S(2)}) %collective-permute-start.15) | collective-permute-done | bytes 65568 | tf_op jit(solution)/shard_map/while/body/eval_jaxpr/ppermute | solution.py:27
  362.0 4.0 collective-permute-done.21
  381.7 57.2 %collective-permute-start.29 = (f32[128,4,16,128]{3,2,1,0:T(8,128)}, f32[128,4,16,128]{3,2,1,0:T(8,128)S(1)}, u32[]{:S(2)}, u32[]{:S(2)}) collective-permute-start(f32[128,4,16,128]{3,2,1,0:T(8,128)} %get-tuple-element.978), channel_id=1, source_target_pairs={{16,0},{24,8},{32,16},{40,24},{48,32},{56,40},{64,48},{72,56},{80,... | collective-permute-start | bytes 12582920 | tf_op jit(solution)/shard_map/ppermute | solution.py:36
  439.0 46.3 %collective-permute-done.29 = f32[128,4,16,128]{3,2,1,0:T(8,128)S(1)} collective-permute-done((f32[128,4,16,128]{3,2,1,0:T(8,128)}, f32[128,4,16,128]{3,2,1,0:T(8,128)S(1)}, u32[]{:S(2)}, u32[]{:S(2)}) %collective-permute-start.29) | collective-permute-done | bytes 4194336 | tf_op jit(solution)/shard_map/ppermute | solution.py:36
  485.3 8.7 %add_add_fusion = f32[128,4,16,128]{3,2,1,0:T(8,128)} fusion(f32[128,4,16,128]{3,2,1,0:T(8,128)S(1)} %collective-permute-done.29, f32[128,4,16,128]{3,2,1,0:T(8,128)} %get-tuple-element.977, f32[128,4,16,128]{3,2,1,0:T(8,128)} %get-tuple-element.975, f32[128,4,16,128]{3,2,1,0:T(8,128)} %collective-permute-done.27), kind=kLoop, calls=%fused_computation.446 | loop fusion | flops 3145728 | bytes 20971520 | tf_op jit(solution)/shard_map/add | solution.py:105
  (218 shorter events, 222.6 us)
Async XLA Ops:
  0.0 79.3 %collective-permute-start.24 = (bf16[128,4,16,128]{3,2,1,0:T(8,128)(2,1)}, bf16[128,4,16,128]{3,2,1,0:T(8,128)(2,1)}, u32[]{:S(2)}, u32[]{:S(2)}) collective-permute-start(bf16[128,4,16,128]{3,2,1,0:T(8,128)(2,1)} %param.8), channel_id=1, source_target_pairs={{248,0},{0,8},{8,16},{16,24},{24,32},{32,40},{40,48},{48,56},{56,6... | collective-permute-start | bytes 6291464 | tf_op jit(solution)/shard_map/ppermute | solution.py:36
  0.0 230.3 %collective-permute-start.28 = (bf16[128,4,16,128]{3,2,1,0:T(8,128)(2,1)}, bf16[128,4,16,128]{3,2,1,0:T(8,128)(2,1)S(1)}, u32[]{:S(2)}, u32[]{:S(2)}) collective-permute-start(bf16[128,4,16,128]{3,2,1,0:T(8,128)(2,1)} %param.8), channel_id=1, source_target_pairs={{240,0},{248,8},{0,16},{8,24},{16,32},{24,40},{32,48},{40,56},{48,... | collective-permute-start | bytes 6291464 | tf_op jit(solution)/shard_map/ppermute | solution.py:36
  2.7 75.1 %collective-permute-start.26 = (f32[2,16,128]{2,1,0:T(8,128)S(1)}, f32[2,16,128]{2,1,0:T(8,128)S(1)}, u32[]{:S(2)}, u32[]{:S(2)}) collective-permute-start(f32[2,16,128]{2,1,0:T(8,128)S(1)} %get-tuple-element.1208), channel_id=1, source_target_pairs={{1,0},{2,1},{3,2},{4,3},{5,4},{6,5},{7,6},{9,8},{10,9},{11,10},{12... | collective-permute-start | bytes 49160 | tf_op jit(solution)/shard_map/ppermute | solution.py:28
  7.6 69.4 %collective-permute-start.25 = (f32[2,16,128]{2,1,0:T(8,128)S(1)}, f32[2,16,128]{2,1,0:T(8,128)S(1)}, u32[]{:S(2)}, u32[]{:S(2)}) collective-permute-start(f32[2,16,128]{2,1,0:T(8,128)S(1)} %get-tuple-element.1209), channel_id=1, source_target_pairs={{0,1},{1,2},{2,3},{3,4},{4,5},{5,6},{6,7},{8,9},{9,10},{10,11},{11... | collective-permute-start | bytes 49160 | tf_op jit(solution)/shard_map/ppermute | solution.py:27
  84.4 12.5 %collective-permute-start.1 = (bf16[8,2,16,128]{3,2,1,0:T(8,128)(2,1)S(1)}, bf16[8,2,16,128]{3,2,1,0:T(8,128)(2,1)S(1)}, u32[]{:S(2)}, u32[]{:S(2)}) collective-permute-start(bf16[8,2,16,128]{3,2,1,0:T(8,128)(2,1)S(1)} %broadcast.402), channel_id=1, source_target_pairs={{0,1},{1,2},{2,3},{3,4},{4,5},{5,6},{6,7},{8,9},{9,10},{10,11},{11... | collective-permute-start | bytes 196616 | tf_op jit(solution)/shard_map/while/body/eval_jaxpr/ppermute | solution.py:27
  86.3 10.6 %collective-permute-start = (bf16[8,2,16,128]{3,2,1,0:T(8,128)(2,1)S(1)}, bf16[8,2,16,128]{3,2,1,0:T(8,128)(2,1)S(1)}, u32[]{:S(2)}, u32[]{:S(2)}) collective-permute-start(bf16[8,2,16,128]{3,2,1,0:T(8,128)(2,1)S(1)} %broadcast.402), channel_id=1, source_target_pairs={{1,0},{2,1},{3,2},{4,3},{5,4},{6,5},{7,6},{9,8},{10,9},{11,10},{12... | collective-permute-start | bytes 196616 | tf_op jit(solution)/shard_map/while/body/eval_jaxpr/ppermute | solution.py:28
  101.2 8.3 %collective-permute-start.3 = (bf16[8,2,16,128]{3,2,1,0:T(8,128)(2,1)S(1)}, bf16[8,2,16,128]{3,2,1,0:T(8,128)(2,1)S(1)}, u32[]{:S(2)}, u32[]{:S(2)}) collective-permute-start(bf16[8,2,16,128]{3,2,1,0:T(8,128)(2,1)S(1)} %get-tuple-element.1497), channel_id=1, source_target_pairs={{0,1},{1,2},{2,3},{3,4},{4,5},{5,6},{6,7},{8,9},{9,10},{10,11},{11... | collective-permute-start | bytes 196616 | tf_op jit(solution)/shard_map/while/body/eval_jaxpr/ppermute | solution.py:27
  111.9 8.3 %collective-permute-start.5 = (bf16[8,2,16,128]{3,2,1,0:T(8,128)(2,1)S(1)}, bf16[8,2,16,128]{3,2,1,0:T(8,128)(2,1)S(1)}, u32[]{:S(2)}, u32[]{:S(2)}) collective-permute-start(bf16[8,2,16,128]{3,2,1,0:T(8,128)(2,1)S(1)} %get-tuple-element.1501), channel_id=1, source_target_pairs={{0,1},{1,2},{2,3},{3,4},{4,5},{5,6},{6,7},{8,9},{9,10},{10,11},{11... | collective-permute-start | bytes 196616 | tf_op jit(solution)/shard_map/while/body/eval_jaxpr/ppermute | solution.py:27
  122.6 8.3 %collective-permute-start.7 = (bf16[8,2,16,128]{3,2,1,0:T(8,128)(2,1)S(1)}, bf16[8,2,16,128]{3,2,1,0:T(8,128)(2,1)S(1)}, u32[]{:S(2)}, u32[]{:S(2)}) collective-permute-start(bf16[8,2,16,128]{3,2,1,0:T(8,128)(2,1)S(1)} %get-tuple-element.1505), channel_id=1, source_target_pairs={{0,1},{1,2},{2,3},{3,4},{4,5},{5,6},{6,7},{8,9},{9,10},{10,11},{11... | collective-permute-start | bytes 196616 | tf_op jit(solution)/shard_map/while/body/eval_jaxpr/ppermute | solution.py:27
  133.2 8.3 %collective-permute-start.9 = (bf16[8,2,16,128]{3,2,1,0:T(8,128)(2,1)S(1)}, bf16[8,2,16,128]{3,2,1,0:T(8,128)(2,1)S(1)}, u32[]{:S(2)}, u32[]{:S(2)}) collective-permute-start(bf16[8,2,16,128]{3,2,1,0:T(8,128)(2,1)S(1)} %get-tuple-element.1509), channel_id=1, source_target_pairs={{0,1},{1,2},{2,3},{3,4},{4,5},{5,6},{6,7},{8,9},{9,10},{10,11},{11... | collective-permute-start | bytes 196616 | tf_op jit(solution)/shard_map/while/body/eval_jaxpr/ppermute | solution.py:27
  143.9 8.3 %collective-permute-start.11 = (bf16[8,2,16,128]{3,2,1,0:T(8,128)(2,1)S(1)}, bf16[8,2,16,128]{3,2,1,0:T(8,128)(2,1)S(1)}, u32[]{:S(2)}, u32[]{:S(2)}) collective-permute-start(bf16[8,2,16,128]{3,2,1,0:T(8,128)(2,1)S(1)} %get-tuple-element.1513), channel_id=1, source_target_pairs={{0,1},{1,2},{2,3},{3,4},{4,5},{5,6},{6,7},{8,9},{9,10},{10,11},{11... | collective-permute-start | bytes 196616 | tf_op jit(solution)/shard_map/while/body/eval_jaxpr/ppermute | solution.py:27
  157.2 12.5 %collective-permute-start.1 = (bf16[8,2,16,128]{3,2,1,0:T(8,128)(2,1)S(1)}, bf16[8,2,16,128]{3,2,1,0:T(8,128)(2,1)S(1)}, u32[]{:S(2)}, u32[]{:S(2)}) collective-permute-start(bf16[8,2,16,128]{3,2,1,0:T(8,128)(2,1)S(1)} %broadcast.402), channel_id=1, source_target_pairs={{0,1},{1,2},{2,3},{3,4},{4,5},{5,6},{6,7},{8,9},{9,10},{10,11},{11... | collective-permute-start | bytes 196616 | tf_op jit(solution)/shard_map/while/body/eval_jaxpr/ppermute | solution.py:27
  159.2 10.6 %collective-permute-start = (bf16[8,2,16,128]{3,2,1,0:T(8,128)(2,1)S(1)}, bf16[8,2,16,128]{3,2,1,0:T(8,128)(2,1)S(1)}, u32[]{:S(2)}, u32[]{:S(2)}) collective-permute-start(bf16[8,2,16,128]{3,2,1,0:T(8,128)(2,1)S(1)} %broadcast.402), channel_id=1, source_target_pairs={{1,0},{2,1},{3,2},{4,3},{5,4},{6,5},{7,6},{9,8},{10,9},{11,10},{12... | collective-permute-start | bytes 196616 | tf_op jit(solution)/shard_map/while/body/eval_jaxpr/ppermute | solution.py:28
  174.1 8.5 %collective-permute-start.3 = (bf16[8,2,16,128]{3,2,1,0:T(8,128)(2,1)S(1)}, bf16[8,2,16,128]{3,2,1,0:T(8,128)(2,1)S(1)}, u32[]{:S(2)}, u32[]{:S(2)}) collective-permute-start(bf16[8,2,16,128]{3,2,1,0:T(8,128)(2,1)S(1)} %get-tuple-element.1497), channel_id=1, source_target_pairs={{0,1},{1,2},{2,3},{3,4},{4,5},{5,6},{6,7},{8,9},{9,10},{10,11},{11... | collective-permute-start | bytes 196616 | tf_op jit(solution)/shard_map/while/body/eval_jaxpr/ppermute | solution.py:27
  206.3 8.3 %collective-permute-start.9 = (bf16[8,2,16,128]{3,2,1,0:T(8,128)(2,1)S(1)}, bf16[8,2,16,128]{3,2,1,0:T(8,128)(2,1)S(1)}, u32[]{:S(2)}, u32[]{:S(2)}) collective-permute-start(bf16[8,2,16,128]{3,2,1,0:T(8,128)(2,1)S(1)} %get-tuple-element.1509), channel_id=1, source_target_pairs={{0,1},{1,2},{2,3},{3,4},{4,5},{5,6},{6,7},{8,9},{9,10},{10,11},{11... | collective-permute-start | bytes 196616 | tf_op jit(solution)/shard_map/while/body/eval_jaxpr/ppermute | solution.py:27
  230.3 208.7 %collective-permute-start.27 = (f32[128,4,16,128]{3,2,1,0:T(8,128)}, f32[128,4,16,128]{3,2,1,0:T(8,128)}, u32[]{:S(2)}, u32[]{:S(2)}) collective-permute-start(f32[128,4,16,128]{3,2,1,0:T(8,128)} %get-tuple-element.976), channel_id=1, source_target_pairs={{8,0},{16,8},{24,16},{32,24},{40,32},{48,40},{56,48},{64,56},{72,6... | collective-permute-start | bytes 12582920 | tf_op jit(solution)/shard_map/ppermute | solution.py:36
  235.4 10.9 %collective-permute-start.13 = (bf16[8,2,16,128]{3,2,1,0:T(8,128)(2,1)S(1)}, bf16[8,2,16,128]{3,2,1,0:T(8,128)(2,1)S(1)}, u32[]{:S(2)}, u32[]{:S(2)}) collective-permute-start(bf16[8,2,16,128]{3,2,1,0:T(8,128)(2,1)S(1)} %broadcast.410), channel_id=1, source_target_pairs={{0,1},{1,2},{2,3},{3,4},{4,5},{5,6},{6,7},{8,9},{9,10},{10,11},{11... | collective-permute-start | bytes 196616 | tf_op jit(solution)/shard_map/while/body/eval_jaxpr/ppermute | solution.py:27
  237.3 9.0 %collective-permute-start.12 = (bf16[8,2,16,128]{3,2,1,0:T(8,128)(2,1)S(1)}, bf16[8,2,16,128]{3,2,1,0:T(8,128)(2,1)S(1)}, u32[]{:S(2)}, u32[]{:S(2)}) collective-permute-start(bf16[8,2,16,128]{3,2,1,0:T(8,128)(2,1)S(1)} %broadcast.410), channel_id=1, source_target_pairs={{1,0},{2,1},{3,2},{4,3},{5,4},{6,5},{7,6},{9,8},{10,9},{11,10},{12... | collective-permute-start | bytes 196616 | tf_op jit(solution)/shard_map/while/body/eval_jaxpr/ppermute | solution.py:28
  284.3 8.3 %collective-permute-start.21 = (bf16[8,2,16,128]{3,2,1,0:T(8,128)(2,1)S(1)}, bf16[8,2,16,128]{3,2,1,0:T(8,128)(2,1)S(1)}, u32[]{:S(2)}, u32[]{:S(2)}) collective-permute-start(bf16[8,2,16,128]{3,2,1,0:T(8,128)(2,1)S(1)} %get-tuple-element.1555), channel_id=1, source_target_pairs={{0,1},{1,2},{2,3},{3,4},{4,5},{5,6},{6,7},{8,9},{9,10},{10,11},{11... | collective-permute-start | bytes 196616 | tf_op jit(solution)/shard_map/while/body/eval_jaxpr/ppermute | solution.py:27
  308.3 10.9 %collective-permute-start.13 = (bf16[8,2,16,128]{3,2,1,0:T(8,128)(2,1)S(1)}, bf16[8,2,16,128]{3,2,1,0:T(8,128)(2,1)S(1)}, u32[]{:S(2)}, u32[]{:S(2)}) collective-permute-start(bf16[8,2,16,128]{3,2,1,0:T(8,128)(2,1)S(1)} %broadcast.410), channel_id=1, source_target_pairs={{0,1},{1,2},{2,3},{3,4},{4,5},{5,6},{6,7},{8,9},{9,10},{10,11},{11... | collective-permute-start | bytes 196616 | tf_op jit(solution)/shard_map/while/body/eval_jaxpr/ppermute | solution.py:27
  310.2 9.0 %collective-permute-start.12 = (bf16[8,2,16,128]{3,2,1,0:T(8,128)(2,1)S(1)}, bf16[8,2,16,128]{3,2,1,0:T(8,128)(2,1)S(1)}, u32[]{:S(2)}, u32[]{:S(2)}) collective-permute-start(bf16[8,2,16,128]{3,2,1,0:T(8,128)(2,1)S(1)} %broadcast.410), channel_id=1, source_target_pairs={{1,0},{2,1},{3,2},{4,3},{5,4},{6,5},{7,6},{9,8},{10,9},{11,10},{12... | collective-permute-start | bytes 196616 | tf_op jit(solution)/shard_map/while/body/eval_jaxpr/ppermute | solution.py:28
  325.3 8.7 %collective-permute-start.15 = (bf16[8,2,16,128]{3,2,1,0:T(8,128)(2,1)S(1)}, bf16[8,2,16,128]{3,2,1,0:T(8,128)(2,1)S(1)}, u32[]{:S(2)}, u32[]{:S(2)}) collective-permute-start(bf16[8,2,16,128]{3,2,1,0:T(8,128)(2,1)S(1)} %get-tuple-element.1543), channel_id=1, source_target_pairs={{0,1},{1,2},{2,3},{3,4},{4,5},{5,6},{6,7},{8,9},{9,10},{10,11},{11... | collective-permute-start | bytes 196616 | tf_op jit(solution)/shard_map/while/body/eval_jaxpr/ppermute | solution.py:27
  357.7 8.3 %collective-permute-start.21 = (bf16[8,2,16,128]{3,2,1,0:T(8,128)(2,1)S(1)}, bf16[8,2,16,128]{3,2,1,0:T(8,128)(2,1)S(1)}, u32[]{:S(2)}, u32[]{:S(2)}) collective-permute-start(bf16[8,2,16,128]{3,2,1,0:T(8,128)(2,1)S(1)} %get-tuple-element.1555), channel_id=1, source_target_pairs={{0,1},{1,2},{2,3},{3,4},{4,5},{5,6},{6,7},{8,9},{9,10},{10,11},{11... | collective-permute-start | bytes 196616 | tf_op jit(solution)/shard_map/while/body/eval_jaxpr/ppermute | solution.py:27
  381.7 103.6 %collective-permute-start.29 = (f32[128,4,16,128]{3,2,1,0:T(8,128)}, f32[128,4,16,128]{3,2,1,0:T(8,128)S(1)}, u32[]{:S(2)}, u32[]{:S(2)}) collective-permute-start(f32[128,4,16,128]{3,2,1,0:T(8,128)} %get-tuple-element.978), channel_id=1, source_target_pairs={{16,0},{24,8},{32,16},{40,24},{48,32},{56,40},{64,48},{72,56},{80,... | collective-permute-start | bytes 12582920 | tf_op jit(solution)/shard_map/ppermute | solution.py:36
  (30 other events, 210.0 us)
where the time goes:
time: 499 us; the launch traced here: 494 us
  starting transfers between devices  218 us (44%)
  waiting for transfers between devices  204 us (41%)
  other arithmetic  42.1 us (8%)
  local copies, waits for them, and re-layouts  28.8 us (6%)
    ppermute x25, waiting for transfers between devices, with_halo(): before = lax.ppermute(last, axis, up)  153 us
    ppermute x25, starting transfers between devices, with_halo(): before = lax.ppermute(last, axis, up)  80.4 us
    ppermute x25, starting transfers between devices, with_halo(): after = lax.ppermute(leading, axis, down)  78 us
    ppermute x4, starting transfers between devices, shifted_2(): return lax.ppermute(block, axis, route)  59.2 us
    ppermute x4, waiting for transfers between devices, shifted_2(): return lax.ppermute(block, axis, route)  46.3 us
    another operation x16, local copies, waits for them, and re-layouts  10.2 us
  transfers between devices with their start and end apart: 54, of which 37 were waited for; matrix products, arithmetic and copies ran while one was open for 13% of the time, Pallas kernels for 0%

commit v1 on v0

v1 whole, which is shorter than its diff:
```python
import math

import jax
import jax.numpy as jnp
from jax import lax
from jax.sharding import PartitionSpec as P

SWEEPS = 6
STEPS = 2

near_weight = 1.0
far_weight = 0.25
screening = 0.02
coupling = 4.0 * math.pi
offsets = (-2, -1, 1, 2)


def with_halo(x, axis, dim, width):
    peers, length = (lax.axis_size(axis), x.shape[dim])
    up = [(i, (i + 1) % peers) for i in range(peers - 1)]
    down = [(j, i) for i, j in up]
    last = lax.slice_in_dim(x, length - width, length, axis=dim)
    leading = lax.slice_in_dim(x, 0, width, axis=dim)
    before = lax.ppermute(last, axis, up)
    after = lax.ppermute(leading, axis, down)
    return jnp.concatenate([before, x, after], axis=dim)


def cycle(block, axis, distance):
    size = lax.axis_size(axis)
    return lax.ppermute(block, axis, [((i - distance) % size, i) for i in range(size)])


def shifted(source, axis_number, offset):
    length = source.shape[axis_number]
    widths = [(0, 0)] * source.ndim
    widths[axis_number] = (2, 2)
    padded = jnp.pad(source, widths)
    return lax.slice_in_dim(padded, 2 + offset, 2 + offset + length, axis=axis_number)


def per_device(orbitals, dielectric, pairs, pair_count):
    planes = orbitals.shape[1]
    slots = pairs.shape[2]
    rim = with_halo(dielectric, "gz", 0, 2)
    center = rim[2 : 2 + planes]
    faces = []
    diagonal = screening * center
    for axis_number in range(3):
        for offset in offsets:
            weight = near_weight if abs(offset) == 1 else far_weight
            if axis_number == 0:
                beyond = rim[2 + offset : 2 + offset + planes]
            else:
                beyond = shifted(center, axis_number, offset)
            face = weight * 0.5 * (center + beyond)
            faces.append((axis_number, offset, face))
            diagonal = diagonal + face

    firsts, seconds, wanted, masks = [], [], [], []
    slot_ids = jnp.arange(slots, dtype=jnp.int32)
    for step in range(1, STEPS + 1):
        chosen = pairs[0, step - 1]
        asked = cycle(chosen[:, 1], "orb", -step)
        wanted.append(asked)
        seconds.append(cycle(orbitals[asked], "orb", step))
        firsts.append(chosen[:, 0])
        masks.append((slot_ids < pair_count[0, step - 1]).astype(jnp.float32))
    first_rows = jnp.concatenate(firsts)
    first = orbitals[first_rows].astype(jnp.float32)
    second = jnp.concatenate(seconds).astype(jnp.float32)
    mask = jnp.concatenate(masks)[:, None, None, None]

    source = coupling * (first * second)
    potential = source / diagonal
    for sweep in range(1, SWEEPS):
        padded = with_halo(potential.astype(jnp.bfloat16), "gz", 1, 2).astype(jnp.float32)
        summed = source
        for axis_number, offset, face in faces:
            if axis_number == 0:
                neighbor = padded[:, 2 + offset : 2 + offset + planes]
            else:
                neighbor = shifted(potential, axis_number + 1, offset)
            summed = summed + face * neighbor
        potential = summed / diagonal
    potential = potential * mask

    back = potential * first
    exchange = jnp.zeros(orbitals.shape, jnp.float32).at[first_rows].add(potential * second)
    for step in range(1, STEPS + 1):
        part = cycle(back[(step - 1) * slots : step * slots], "orb", -step)
        exchange = exchange.at[wanted[step - 1]].add(part)
    return exchange


def solution(mesh):
    placed = (
        P("orb", "gz", None, None),
        P("gz", None, None),
        P("orb", None, None, None),
        P("orb", None),
    )
    return jax.shard_map(
        per_device,
        mesh=mesh,
        in_specs=placed,
        out_specs=P("orb", "gz", None, None),
        check_vma=False,
    )
```

time: 499 us -> 136 us (0.27)
  waiting for transfers between devices: 204 us -> 43.9 us
  starting transfers between devices: 218 us -> 58.1 us
  local copies, waits for them, and re-layouts: 28.8 us -> 7.92 us
  other arithmetic: 42.1 us -> 22.9 us
    ppermute x25 -> x6, waiting for transfers between devices: 153 us -> 20.5 us  [with_halo(): before = lax.ppermute(last, axis, up)]
    ppermute x25 -> x6, starting transfers between devices: 80.4 us -> 11.5 us  [with_halo(): before = lax.ppermute(last, axis, up)]
    ppermute x4 -> x6, starting transfers between devices: 59.2 us -> 8.78 us  [cycle(): lax.ppermute(block, axis, [((i - distance) % size, i) for i in range(size)])]
    ppermute x25 -> x6, starting transfers between devices: 78 us -> 37.8 us  [with_halo(): after = lax.ppermute(leading, axis, down)]
    ppermute x4 -> x6, waiting for transfers between devices: 46.3 us -> 16.5 us  [cycle(): lax.ppermute(block, axis, [((i - distance) % size, i) for i in range(size)])]
    gather x8 -> x3, local copies, waits for them, and re-layouts: 14.1 us -> 1.84 us  [the longest x2 1.19 us: per_device(): seconds.append(cycle(orbitals[asked], 'orb', step))]
    another operation x16 -> x0, local copies, waits for them, and re-layouts: 10.2 us -> none
    add x2 -> x0, other arithmetic: 10.2 us -> none  [the longest x1 8.7 us: per_device(): exchange = exchange + own_part + shifted_2(visit_part, 'orb', -cycle_step)]
  transfers between devices with their start and end apart: 54 -> 18, of which waited for: 37 -> 15; matrix products, arithmetic and copies ran while one was open for 13% -> 11% of each run, Pallas kernels for 0% -> 0%
where the time goes in v1:
time: 136 us; the launch traced here: 133 us
  starting transfers between devices  58.1 us (43%)
  waiting for transfers between devices  43.9 us (32%)
  other arithmetic  22.9 us (17%)
  local copies, waits for them, and re-layouts  7.92 us (6%)
    ppermute x6, starting transfers between devices, with_halo(): after = lax.ppermute(leading, axis, down)  37.8 us
    ppermute x6, waiting for transfers between devices, with_halo(): before = lax.ppermute(last, axis, up)  20.5 us
    ppermute x6, waiting for transfers between devices, cycle(): lax.ppermute(block, axis, [((i - distance) % size, i) for i in range(size)])  16.5 us
    ppermute x6, starting transfers between devices, with_halo(): before = lax.ppermute(last, axis, up)  11.5 us
    ppermute x6, starting transfers between devices, cycle(): lax.ppermute(block, axis, [((i - distance) % size, i) for i in range(size)])  8.78 us
    convert_element_type x5, other arithmetic, per_device(): potential.astype(jnp.bfloat16)  7.42 us
    ppermute x6, waiting for transfers between devices, with_halo(): after = lax.ppermute(leading, axis, down)  6.87 us
    scatter-add x2, other arithmetic, per_device(): exchange = exchange.at[wanted[step - 1]].add(part)  5.99 us
  transfers between devices with their start and end apart: 18, of which 15 were waited for; matrix products, arithmetic and copies ran while one was open for 11% of the time, Pallas kernels for 0%

profile of v1, /device:TPU:2, one launch (start us, length us, event | category | flops | bytes accessed | tf_op | source)
XLA Modules:
  0.0 133.2 jit_solution(5908507208353134366)
XLA Ops:
  0.9 7.4 %collective-permute-start.2 = (s32[16]{0:T(128)S(1)}, s32[16]{0:T(128)S(1)}, u32[]{:S(2)}, u32[]{:S(2)}) collective-permute-start(s32[16]{0:T(128)S(1)} %get-tuple-element.50), channel_id=1, source_target_pairs={{16,0},{24,8},{32,16},{40,24},{48,32},{56,40},{64,48},{72,56},{80,... | collective-permute-start | bytes 200 | tf_op jit(solution)/shard_map/ppermute | solution.py:31
  9.2 5.8 %collective-permute-start.5 = (f32[2,16,128]{2,1,0:T(8,128)S(1)}, f32[2,16,128]{2,1,0:T(8,128)S(1)}, u32[]{:S(2)}, u32[]{:S(2)}) collective-permute-start(f32[2,16,128]{2,1,0:T(8,128)S(1)} %get-tuple-element.42), channel_id=1, source_target_pairs={{1,0},{2,1},{3,2},{4,3},{5,4},{6,5},{7,6},{9,8},{10,9},{11,10},{12... | collective-permute-start | bytes 49160 | tf_op jit(solution)/shard_map/ppermute | solution.py:25
  15.0 1.9 %collective-permute-start.4 = (f32[2,16,128]{2,1,0:T(8,128)S(1)}, f32[2,16,128]{2,1,0:T(8,128)S(1)}, u32[]{:S(2)}, u32[]{:S(2)}) collective-permute-start(f32[2,16,128]{2,1,0:T(8,128)S(1)} %get-tuple-element.43), channel_id=1, source_target_pairs={{0,1},{1,2},{2,3},{3,4},{4,5},{5,6},{6,7},{8,9},{9,10},{10,11},{11... | collective-permute-start | bytes 49160 | tf_op jit(solution)/shard_map/ppermute | solution.py:24
  20.1 2.6 %collective-permute-done.4 = f32[2,16,128]{2,1,0:T(8,128)S(1)} collective-permute-done((f32[2,16,128]{2,1,0:T(8,128)S(1)}, f32[2,16,128]{2,1,0:T(8,128)S(1)}, u32[]{:S(2)}, u32[]{:S(2)}) %collective-permute-start.4) | collective-permute-done | bytes 16416 | tf_op jit(solution)/shard_map/ppermute | solution.py:24
  22.9 7.7 %collective-permute-done.1 = bf16[16,4,16,128]{3,2,1,0:T(8,128)(2,1)S(1)} collective-permute-done((bf16[16,4,16,128]{3,2,1,0:T(8,128)(2,1)S(1)}, bf16[16,4,16,128]{3,2,1,0:T(8,128)(2,1)S(1)}, u32[]{:S(2)}, u32[]{:S(2)}) %collective-permute-start.1) | collective-permute-done | bytes 262176 | tf_op jit(solution)/shard_map/ppermute | solution.py:31
  32.1 1.9 %collective-permute-start.6 = (bf16[32,2,16,128]{3,2,1,0:T(8,128)(2,1)S(1)}, bf16[32,2,16,128]{3,2,1,0:T(8,128)(2,1)S(1)}, u32[]{:S(2)}, u32[]{:S(2)}) collective-permute-start(bf16[32,2,16,128]{3,2,1,0:T(8,128)(2,1)S(1)} %get-tuple-element.27), channel_id=1, source_target_pairs={{0,1},{1,2},{2,3},{3,4},{4,5},{5,6},{6,7},{8,9},{9,10},{10,11},{11... | collective-permute-start | bytes 786440 | tf_op jit(solution)/shard_map/ppermute | solution.py:24
  34.0 6.0 %collective-permute-start.7 = (bf16[32,2,16,128]{3,2,1,0:T(8,128)(2,1)S(1)}, bf16[32,2,16,128]{3,2,1,0:T(8,128)(2,1)S(1)}, u32[]{:S(2)}, u32[]{:S(2)}) collective-permute-start(bf16[32,2,16,128]{3,2,1,0:T(8,128)(2,1)S(1)} %get-tuple-element.28), channel_id=1, source_target_pairs={{1,0},{2,1},{3,2},{4,3},{5,4},{6,5},{7,6},{9,8},{10,9},{11,10},{12... | collective-permute-start | bytes 786440 | tf_op jit(solution)/shard_map/ppermute | solution.py:25
  40.1 3.8 %collective-permute-done.6 = bf16[32,2,16,128]{3,2,1,0:T(8,128)(2,1)S(1)} collective-permute-done((bf16[32,2,16,128]{3,2,1,0:T(8,128)(2,1)S(1)}, bf16[32,2,16,128]{3,2,1,0:T(8,128)(2,1)S(1)}, u32[]{:S(2)}, u32[]{:S(2)}) %collective-permute-start.6) | collective-permute-done | bytes 262176 | tf_op jit(solution)/shard_map/ppermute | solution.py:24
  49.6 6.5 %collective-permute-start.9 = (bf16[32,2,16,128]{3,2,1,0:T(8,128)(2,1)S(1)}, bf16[32,2,16,128]{3,2,1,0:T(8,128)(2,1)S(1)}, u32[]{:S(2)}, u32[]{:S(2)}) collective-permute-start(bf16[32,2,16,128]{3,2,1,0:T(8,128)(2,1)S(1)} %get-tuple-element.26), channel_id=1, source_target_pairs={{1,0},{2,1},{3,2},{4,3},{5,4},{6,5},{7,6},{9,8},{10,9},{11,10},{12... | collective-permute-start | bytes 786440 | tf_op jit(solution)/shard_map/ppermute | solution.py:25
  56.2 5.0 %collective-permute-done.8 = bf16[32,2,16,128]{3,2,1,0:T(8,128)(2,1)S(1)} collective-permute-done((bf16[32,2,16,128]{3,2,1,0:T(8,128)(2,1)S(1)}, bf16[32,2,16,128]{3,2,1,0:T(8,128)(2,1)S(1)}, u32[]{:S(2)}, u32[]{:S(2)}) %collective-permute-start.8) | collective-permute-done | bytes 262176 | tf_op jit(solution)/shard_map/ppermute | solution.py:24
  64.7 1.9 %collective-permute-start.10 = (bf16[32,2,16,128]{3,2,1,0:T(8,128)(2,1)S(1)}, bf16[32,2,16,128]{3,2,1,0:T(8,128)(2,1)S(1)}, u32[]{:S(2)}, u32[]{:S(2)}) collective-permute-start(bf16[32,2,16,128]{3,2,1,0:T(8,128)(2,1)S(1)} %get-tuple-element.23), channel_id=1, source_target_pairs={{0,1},{1,2},{2,3},{3,4},{4,5},{5,6},{6,7},{8,9},{9,10},{10,11},{11... | collective-permute-start | bytes 786440 | tf_op jit(solution)/shard_map/ppermute | solution.py:24
  66.7 6.5 %collective-permute-start.11 = (bf16[32,2,16,128]{3,2,1,0:T(8,128)(2,1)S(1)}, bf16[32,2,16,128]{3,2,1,0:T(8,128)(2,1)S(1)}, u32[]{:S(2)}, u32[]{:S(2)}) collective-permute-start(bf16[32,2,16,128]{3,2,1,0:T(8,128)(2,1)S(1)} %get-tuple-element.24), channel_id=1, source_target_pairs={{1,0},{2,1},{3,2},{4,3},{5,4},{6,5},{7,6},{9,8},{10,9},{11,10},{12... | collective-permute-start | bytes 786440 | tf_op jit(solution)/shard_map/ppermute | solution.py:25
  73.2 4.5 %collective-permute-done.10 = bf16[32,2,16,128]{3,2,1,0:T(8,128)(2,1)S(1)} collective-permute-done((bf16[32,2,16,128]{3,2,1,0:T(8,128)(2,1)S(1)}, bf16[32,2,16,128]{3,2,1,0:T(8,128)(2,1)S(1)}, u32[]{:S(2)}, u32[]{:S(2)}) %collective-permute-start.10) | collective-permute-done | bytes 262176 | tf_op jit(solution)/shard_map/ppermute | solution.py:24
  80.9 1.9 %collective-permute-start.12 = (bf16[32,2,16,128]{3,2,1,0:T(8,128)(2,1)S(1)}, bf16[32,2,16,128]{3,2,1,0:T(8,128)(2,1)S(1)}, u32[]{:S(2)}, u32[]{:S(2)}) collective-permute-start(bf16[32,2,16,128]{3,2,1,0:T(8,128)(2,1)S(1)} %get-tuple-element.21), channel_id=1, source_target_pairs={{0,1},{1,2},{2,3},{3,4},{4,5},{5,6},{6,7},{8,9},{9,10},{10,11},{11... | collective-permute-start | bytes 786440 | tf_op jit(solution)/shard_map/ppermute | solution.py:24
  82.8 6.5 %collective-permute-start.13 = (bf16[32,2,16,128]{3,2,1,0:T(8,128)(2,1)S(1)}, bf16[32,2,16,128]{3,2,1,0:T(8,128)(2,1)S(1)}, u32[]{:S(2)}, u32[]{:S(2)}) collective-permute-start(bf16[32,2,16,128]{3,2,1,0:T(8,128)(2,1)S(1)} %get-tuple-element.22), channel_id=1, source_target_pairs={{1,0},{2,1},{3,2},{4,3},{5,4},{6,5},{7,6},{9,8},{10,9},{11,10},{12... | collective-permute-start | bytes 786440 | tf_op jit(solution)/shard_map/ppermute | solution.py:25
  89.3 3.7 %collective-permute-done.12 = bf16[32,2,16,128]{3,2,1,0:T(8,128)(2,1)S(1)} collective-permute-done((bf16[32,2,16,128]{3,2,1,0:T(8,128)(2,1)S(1)}, bf16[32,2,16,128]{3,2,1,0:T(8,128)(2,1)S(1)}, u32[]{:S(2)}, u32[]{:S(2)}) %collective-permute-start.12) | collective-permute-done | bytes 262176 | tf_op jit(solution)/shard_map/ppermute | solution.py:24
  98.1 6.5 %collective-permute-start.15 = (bf16[32,2,16,128]{3,2,1,0:T(8,128)(2,1)S(1)}, bf16[32,2,16,128]{3,2,1,0:T(8,128)(2,1)S(1)}, u32[]{:S(2)}, u32[]{:S(2)}) collective-permute-start(bf16[32,2,16,128]{3,2,1,0:T(8,128)(2,1)S(1)} %get-tuple-element.20), channel_id=1, source_target_pairs={{1,0},{2,1},{3,2},{4,3},{5,4},{6,5},{7,6},{9,8},{10,9},{11,10},{12... | collective-permute-start | bytes 786440 | tf_op jit(solution)/shard_map/ppermute | solution.py:25
  108.8 2.3 %convert_multiply_fusion.2 = (f32[32,4,16,128]{3,2,1,0:T(8,128)S(1)}, f32[32,4,16,128]{3,2,1,0:T(8,128)S(1)}) fusion(bf16[32,4,16,128]{3,2,1,0:T(8,128)(2,1)S(1)} %gather_fusion, f32[32]{0:T(128)S(1)} %add_convert_fusion, f32[4,16,128]{2,1,0:T(8,128)S(1)} %get-tuple-element.31, f32[4,16,128]{2,1,0:T(8,128)S(1)} %get-tuple-element.40, ...), kind=kLoop, calls=%fused_computation.48 | loop fusion | flops 8388608 | bytes 8814720 | tf_op jit(solution)/shard_map/mul | solution.py:88
  112.3 2.5 %broadcast_in_dim.6 = f32[128,4,16,128]{3,2,1,0:T(8,128)} broadcast(f32[]{:T(128)} %constant.7.clone.1), dimensions={} | broadcast | bytes 4194308 | tf_op jit(solution)/shard_map/broadcast_in_dim | solution.py:89
  114.8 4.8 %scatter_fusion = f32[128,4,16,128]{3,2,1,0:T(8,128)} fusion(f32[128,4,16,128]{3,2,1,0:T(8,128)} %broadcast_in_dim.6, s32[32]{0:T(128)S(1)} %fusion.127, f32[32,4,16,128]{3,2,1,0:T(8,128)S(1)} %convert_multiply_fusion), kind=kCustom, calls=%fused_computation.3 | custom fusion | flops 262144 | bytes 3145856 | tf_op jit(solution)/shard_map/scatter-add | solution.py:89
  119.6 5.0 %collective-permute-done.16 = f32[16,4,16,128]{3,2,1,0:T(8,128)} collective-permute-done((f32[16,4,16,128]{3,2,1,0:T(8,128)}, f32[16,4,16,128]{3,2,1,0:T(8,128)}, u32[]{:S(2)}, u32[]{:S(2)}) %collective-permute-start.16) | collective-permute-done | bytes 524320 | tf_op jit(solution)/shard_map/ppermute | solution.py:31
  124.6 3.0 %scatter_fusion.1 = f32[128,4,16,128]{3,2,1,0:T(8,128)} fusion(f32[128,4,16,128]{3,2,1,0:T(8,128)} %scatter_fusion, s32[16]{0:T(128)S(1)} %compare_select_fusion.1, f32[16,4,16,128]{3,2,1,0:T(8,128)} %collective-permute-done.16), kind=kCustom, calls=%fused_computation.4 | custom fusion | flops 131072 | bytes 1572928 | tf_op jit(solution)/shard_map/scatter-add | solution.py:92
  127.6 2.6 %collective-permute-done.17 = f32[16,4,16,128]{3,2,1,0:T(8,128)} collective-permute-done((f32[16,4,16,128]{3,2,1,0:T(8,128)}, f32[16,4,16,128]{3,2,1,0:T(8,128)}, u32[]{:S(2)}, u32[]{:S(2)}) %collective-permute-start.17) | collective-permute-done | bytes 524320 | tf_op jit(solution)/shard_map/ppermute | solution.py:31
  130.2 3.0 %scatter_fusion.2 = f32[128,4,16,128]{3,2,1,0:T(8,128)} fusion(f32[128,4,16,128]{3,2,1,0:T(8,128)} %scatter_fusion.1, s32[16]{0:T(128)S(1)} %compare_select_fusion, f32[16,4,16,128]{3,2,1,0:T(8,128)} %collective-permute-done.17), kind=kCustom, calls=%fused_computation.5 | custom fusion | flops 131072 | bytes 1572928 | tf_op jit(solution)/shard_map/scatter-add | solution.py:92
  (59 shorter events, 29.4 us)
Async XLA Ops:
  0.0 17.0 %copy-start = (bf16[128,4,16,128]{3,2,1,0:T(8,128)(2,1)S(1)}, bf16[128,4,16,128]{3,2,1,0:T(8,128)(2,1)}, u32[]{:S(2)}) copy-start(bf16[128,4,16,128]{3,2,1,0:T(8,128)(2,1)} %param.4) | copy-start | bytes 6291460
  0.0 22.7 %copy-start.1 = (f32[4,16,128]{2,1,0:T(8,128)S(1)}, f32[4,16,128]{2,1,0:T(8,128)}, u32[]{:S(2)}) copy-start(f32[4,16,128]{2,1,0:T(8,128)} %param.5) | copy-start | bytes 98308
  0.9 16.8 %collective-permute-start.2 = (s32[16]{0:T(128)S(1)}, s32[16]{0:T(128)S(1)}, u32[]{:S(2)}, u32[]{:S(2)}) collective-permute-start(s32[16]{0:T(128)S(1)} %get-tuple-element.50), channel_id=1, source_target_pairs={{16,0},{24,8},{32,16},{40,24},{48,32},{56,40},{64,48},{72,56},{80,... | collective-permute-start | bytes 200 | tf_op jit(solution)/shard_map/ppermute | solution.py:31
  8.3 9.4 %collective-permute-start = (s32[16]{0:T(128)S(1)}, s32[16]{0:T(128)S(1)}, u32[]{:S(2)}, u32[]{:S(2)}) collective-permute-start(s32[16]{0:T(128)S(1)} %get-tuple-element.48), channel_id=1, source_target_pairs={{8,0},{16,8},{24,16},{32,24},{40,32},{48,40},{56,48},{64,56},{72,6... | collective-permute-start | bytes 200 | tf_op jit(solution)/shard_map/ppermute | solution.py:31
  9.2 13.5 %collective-permute-start.5 = (f32[2,16,128]{2,1,0:T(8,128)S(1)}, f32[2,16,128]{2,1,0:T(8,128)S(1)}, u32[]{:S(2)}, u32[]{:S(2)}) collective-permute-start(f32[2,16,128]{2,1,0:T(8,128)S(1)} %get-tuple-element.42), channel_id=1, source_target_pairs={{1,0},{2,1},{3,2},{4,3},{5,4},{6,5},{7,6},{9,8},{10,9},{11,10},{12... | collective-permute-start | bytes 49160 | tf_op jit(solution)/shard_map/ppermute | solution.py:25
  15.0 7.7 %collective-permute-start.4 = (f32[2,16,128]{2,1,0:T(8,128)S(1)}, f32[2,16,128]{2,1,0:T(8,128)S(1)}, u32[]{:S(2)}, u32[]{:S(2)}) collective-permute-start(f32[2,16,128]{2,1,0:T(8,128)S(1)} %get-tuple-element.43), channel_id=1, source_target_pairs={{0,1},{1,2},{2,3},{3,4},{4,5},{5,6},{6,7},{8,9},{9,10},{10,11},{11... | collective-permute-start | bytes 49160 | tf_op jit(solution)/shard_map/ppermute | solution.py:24
  18.9 11.7 %collective-permute-start.1 = (bf16[16,4,16,128]{3,2,1,0:T(8,128)(2,1)S(1)}, bf16[16,4,16,128]{3,2,1,0:T(8,128)(2,1)S(1)}, u32[]{:S(2)}, u32[]{:S(2)}) collective-permute-start(bf16[16,4,16,128]{3,2,1,0:T(8,128)(2,1)S(1)} %gather_fusion.1), channel_id=1, source_target_pairs={{248,0},{0,8},{8,16},{16,24},{24,32},{32,40},{40,48},{48,56},{56,6... | collective-permute-start | bytes 786440 | tf_op jit(solution)/shard_map/ppermute | solution.py:31
  19.1 12.8 %collective-permute-start.3 = (bf16[16,4,16,128]{3,2,1,0:T(8,128)(2,1)S(1)}, bf16[16,4,16,128]{3,2,1,0:T(8,128)(2,1)S(1)}, u32[]{:S(2)}, u32[]{:S(2)}) collective-permute-start(bf16[16,4,16,128]{3,2,1,0:T(8,128)(2,1)S(1)} %gather_fusion.2), channel_id=1, source_target_pairs={{240,0},{248,8},{0,16},{8,24},{16,32},{24,40},{32,48},{40,56},{48,... | collective-permute-start | bytes 786440 | tf_op jit(solution)/shard_map/ppermute | solution.py:31
  32.1 11.8 %collective-permute-start.6 = (bf16[32,2,16,128]{3,2,1,0:T(8,128)(2,1)S(1)}, bf16[32,2,16,128]{3,2,1,0:T(8,128)(2,1)S(1)}, u32[]{:S(2)}, u32[]{:S(2)}) collective-permute-start(bf16[32,2,16,128]{3,2,1,0:T(8,128)(2,1)S(1)} %get-tuple-element.27), channel_id=1, source_target_pairs={{0,1},{1,2},{2,3},{3,4},{4,5},{5,6},{6,7},{8,9},{9,10},{10,11},{11... | collective-permute-start | bytes 786440 | tf_op jit(solution)/shard_map/ppermute | solution.py:24
  34.0 11.7 %collective-permute-start.7 = (bf16[32,2,16,128]{3,2,1,0:T(8,128)(2,1)S(1)}, bf16[32,2,16,128]{3,2,1,0:T(8,128)(2,1)S(1)}, u32[]{:S(2)}, u32[]{:S(2)}) collective-permute-start(bf16[32,2,16,128]{3,2,1,0:T(8,128)(2,1)S(1)} %get-tuple-element.28), channel_id=1, source_target_pairs={{1,0},{2,1},{3,2},{4,3},{5,4},{6,5},{7,6},{9,8},{10,9},{11,10},{12... | collective-permute-start | bytes 786440 | tf_op jit(solution)/shard_map/ppermute | solution.py:25
  47.7 13.5 %collective-permute-start.8 = (bf16[32,2,16,128]{3,2,1,0:T(8,128)(2,1)S(1)}, bf16[32,2,16,128]{3,2,1,0:T(8,128)(2,1)S(1)}, u32[]{:S(2)}, u32[]{:S(2)}) collective-permute-start(bf16[32,2,16,128]{3,2,1,0:T(8,128)(2,1)S(1)} %get-tuple-element.25), channel_id=1, source_target_pairs={{0,1},{1,2},{2,3},{3,4},{4,5},{5,6},{6,7},{8,9},{9,10},{10,11},{11... | collective-permute-start | bytes 786440 | tf_op jit(solution)/shard_map/ppermute | solution.py:24
  49.6 13.1 %collective-permute-start.9 = (bf16[32,2,16,128]{3,2,1,0:T(8,128)(2,1)S(1)}, bf16[32,2,16,128]{3,2,1,0:T(8,128)(2,1)S(1)}, u32[]{:S(2)}, u32[]{:S(2)}) collective-permute-start(bf16[32,2,16,128]{3,2,1,0:T(8,128)(2,1)S(1)} %get-tuple-element.26), channel_id=1, source_target_pairs={{1,0},{2,1},{3,2},{4,3},{5,4},{6,5},{7,6},{9,8},{10,9},{11,10},{12... | collective-permute-start | bytes 786440 | tf_op jit(solution)/shard_map/ppermute | solution.py:25
  64.7 13.0 %collective-permute-start.10 = (bf16[32,2,16,128]{3,2,1,0:T(8,128)(2,1)S(1)}, bf16[32,2,16,128]{3,2,1,0:T(8,128)(2,1)S(1)}, u32[]{:S(2)}, u32[]{:S(2)}) collective-permute-start(bf16[32,2,16,128]{3,2,1,0:T(8,128)(2,1)S(1)} %get-tuple-element.23), channel_id=1, source_target_pairs={{0,1},{1,2},{2,3},{3,4},{4,5},{5,6},{6,7},{8,9},{9,10},{10,11},{11... | collective-permute-start | bytes 786440 | tf_op jit(solution)/shard_map/ppermute | solution.py:24
  66.7 12.2 %collective-permute-start.11 = (bf16[32,2,16,128]{3,2,1,0:T(8,128)(2,1)S(1)}, bf16[32,2,16,128]{3,2,1,0:T(8,128)(2,1)S(1)}, u32[]{:S(2)}, u32[]{:S(2)}) collective-permute-start(bf16[32,2,16,128]{3,2,1,0:T(8,128)(2,1)S(1)} %get-tuple-element.24), channel_id=1, source_target_pairs={{1,0},{2,1},{3,2},{4,3},{5,4},{6,5},{7,6},{9,8},{10,9},{11,10},{12... | collective-permute-start | bytes 786440 | tf_op jit(solution)/shard_map/ppermute | solution.py:25
  80.9 12.1 %collective-permute-start.12 = (bf16[32,2,16,128]{3,2,1,0:T(8,128)(2,1)S(1)}, bf16[32,2,16,128]{3,2,1,0:T(8,128)(2,1)S(1)}, u32[]{:S(2)}, u32[]{:S(2)}) collective-permute-start(bf16[32,2,16,128]{3,2,1,0:T(8,128)(2,1)S(1)} %get-tuple-element.21), channel_id=1, source_target_pairs={{0,1},{1,2},{2,3},{3,4},{4,5},{5,6},{6,7},{8,9},{9,10},{10,11},{11... | collective-permute-start | bytes 786440 | tf_op jit(solution)/shard_map/ppermute | solution.py:24
  82.8 11.4 %collective-permute-start.13 = (bf16[32,2,16,128]{3,2,1,0:T(8,128)(2,1)S(1)}, bf16[32,2,16,128]{3,2,1,0:T(8,128)(2,1)S(1)}, u32[]{:S(2)}, u32[]{:S(2)}) collective-permute-start(bf16[32,2,16,128]{3,2,1,0:T(8,128)(2,1)S(1)} %get-tuple-element.22), channel_id=1, source_target_pairs={{1,0},{2,1},{3,2},{4,3},{5,4},{6,5},{7,6},{9,8},{10,9},{11,10},{12... | collective-permute-start | bytes 786440 | tf_op jit(solution)/shard_map/ppermute | solution.py:25
  94.4 10.3 %copy-start.2 = (s32[1,2]{1,0:T(1,128)S(1)}, s32[1,2]{1,0:T(1,128)}, u32[]{:S(2)}) copy-start(s32[1,2]{1,0:T(1,128)} %param.7) | copy-start | bytes 28
  96.2 11.2 %collective-permute-start.14 = (bf16[32,2,16,128]{3,2,1,0:T(8,128)(2,1)S(1)}, bf16[32,2,16,128]{3,2,1,0:T(8,128)(2,1)S(1)}, u32[]{:S(2)}, u32[]{:S(2)}) collective-permute-start(bf16[32,2,16,128]{3,2,1,0:T(8,128)(2,1)S(1)} %get-tuple-element.19), channel_id=1, source_target_pairs={{0,1},{1,2},{2,3},{3,4},{4,5},{5,6},{6,7},{8,9},{9,10},{10,11},{11... | collective-permute-start | bytes 786440 | tf_op jit(solution)/shard_map/ppermute | solution.py:24
  98.1 10.5 %collective-permute-start.15 = (bf16[32,2,16,128]{3,2,1,0:T(8,128)(2,1)S(1)}, bf16[32,2,16,128]{3,2,1,0:T(8,128)(2,1)S(1)}, u32[]{:S(2)}, u32[]{:S(2)}) collective-permute-start(bf16[32,2,16,128]{3,2,1,0:T(8,128)(2,1)S(1)} %get-tuple-element.20), channel_id=1, source_target_pairs={{1,0},{2,1},{3,2},{4,3},{5,4},{6,5},{7,6},{9,8},{10,9},{11,10},{12... | collective-permute-start | bytes 786440 | tf_op jit(solution)/shard_map/ppermute | solution.py:25
  112.1 12.5 %collective-permute-start.16 = (f32[16,4,16,128]{3,2,1,0:T(8,128)}, f32[16,4,16,128]{3,2,1,0:T(8,128)}, u32[]{:S(2)}, u32[]{:S(2)}) collective-permute-start(f32[16,4,16,128]{3,2,1,0:T(8,128)} %get-tuple-element.18), channel_id=1, source_target_pairs={{8,0},{16,8},{24,16},{32,24},{40,32},{48,40},{56,48},{64,56},{72,6... | collective-permute-start | bytes 1572872 | tf_op jit(solution)/shard_map/ppermute | solution.py:31
  112.1 18.1 %collective-permute-start.17 = (f32[16,4,16,128]{3,2,1,0:T(8,128)}, f32[16,4,16,128]{3,2,1,0:T(8,128)}, u32[]{:S(2)}, u32[]{:S(2)}) collective-permute-start(f32[16,4,16,128]{3,2,1,0:T(8,128)} %get-tuple-element.17), channel_id=1, source_target_pairs={{16,0},{24,8},{32,16},{40,24},{48,32},{56,40},{64,48},{72,56},{80,... | collective-permute-start | bytes 1572872 | tf_op jit(solution)/shard_map/ppermute | solution.py:31

commit v2 on v1

v2 whole, which is shorter than its diff:
```python
import functools
import math

import jax
import jax.numpy as jnp
from jax import lax
from jax.experimental import pallas as pl
from jax.experimental.pallas import tpu as pltpu
from jax.sharding import PartitionSpec as P

SWEEPS = 6
STEPS = 2
ROUNDS = SWEEPS - 1
LANES = 8

near_weight = 1.0
far_weight = 0.25
screening = 0.02
coupling = 4.0 * math.pi
offsets = (-2, -1, 1, 2)
MESH = pl.DeviceIdType.MESH


def step_of(batch):
    return ((batch + 1) // 2) % 2


def half_of(batch):
    return batch // 2


def relax_kernel(
    groups,
    slabs,
    orb_hbm,
    diel,
    pairs,
    count,
    pairs_hbm,
    own_out,
    vis_out,
    asked_out,
    orb,
    asked,
    rim,
    wide,
    face,
    rdiag,
    fwd,
    sec,
    nat,
    base,
    pot,
    up_snd,
    dn_snd,
    lo_rcv,
    hi_rcv,
    ret,
    own,
    load_sem,
    ask_s,
    ask_r,
    asked_sem,
    rim_s,
    rim_r,
    fwd_s,
    fwd_r,
    up_s,
    lo_r,
    dn_s,
    hi_r,
    ret_s,
    ret_r,
    own_sem,
):
    me = lax.axis_index("orb")
    gz = lax.axis_index("gz")
    planes, nx, ny = diel.shape
    batches = sec.shape[0]
    cells = planes * nx

    def group(distance):
        return lax.rem(me + distance + groups, groups)

    load = pltpu.make_async_copy(orb_hbm, orb, load_sem)
    load.start()

    barrier = pltpu.get_barrier_semaphore()
    for distance in (-2, -1, 1, 2):
        pl.semaphore_signal(
            barrier, inc=1, device_id=(group(distance), gz), device_id_type=MESH
        )

    @pl.when(gz > 0)
    def _():
        pl.semaphore_signal(barrier, inc=1, device_id=(me, gz - 1), device_id_type=MESH)

    @pl.when(gz < slabs - 1)
    def _():
        pl.semaphore_signal(barrier, inc=1, device_id=(me, gz + 1), device_id_type=MESH)

    @pl.when((gz == 0) | (gz == slabs - 1))
    def _():
        pl.semaphore_wait(barrier, 5)

    @pl.when((gz > 0) & (gz < slabs - 1))
    def _():
        pl.semaphore_wait(barrier, 6)

    def ask(step):
        return pltpu.make_async_remote_copy(
            src_ref=pairs_hbm.at[0, step],
            dst_ref=asked_out.at[step],
            send_sem=ask_s.at[step],
            recv_sem=ask_r.at[step],
            device_id=(group(-step - 1), gz),
            device_id_type=MESH,
        )

    for step in range(STEPS):
        ask(step).start()

    def rim_up():
        return pltpu.make_async_remote_copy(
            src_ref=diel.at[pl.ds(planes - 2, 2)],
            dst_ref=rim.at[0],
            send_sem=rim_s.at[0],
            recv_sem=rim_r.at[0],
            device_id=(me, gz + 1),
            device_id_type=MESH,
        )

    def rim_down():
        return pltpu.make_async_remote_copy(
            src_ref=diel.at[pl.ds(0, 2)],
            dst_ref=rim.at[1],
            send_sem=rim_s.at[1],
            recv_sem=rim_r.at[1],
            device_id=(me, gz - 1),
            device_id_type=MESH,
        )

    @pl.when(gz < slabs - 1)
    def _():
        rim_up().start()

    @pl.when(gz > 0)
    def _():
        rim_down().start()

    @pl.when(gz == 0)
    def _():
        rim[0] = jnp.zeros(rim.shape[1:], rim.dtype)
        pot[:, :, 0 : 2 * nx] = jnp.zeros((batches, 2, 2 * nx, LANES, ny), jnp.float32)

    @pl.when(gz == slabs - 1)
    def _():
        rim[1] = jnp.zeros(rim.shape[1:], rim.dtype)
        pot[:, :, (planes + 2) * nx :] = jnp.zeros(
            (batches, 2, 2 * nx, LANES, ny), jnp.float32
        )

    load.wait()

    def forward(batch):
        return pltpu.make_async_remote_copy(
            src_ref=fwd.at[batch],
            dst_ref=sec.at[batch],
            send_sem=fwd_s.at[batch],
            recv_sem=fwd_r.at[batch],
            device_id=(group(step_of(batch) + 1), gz),
            device_id_type=MESH,
        )

    def asked_copy(step):
        return pltpu.make_async_copy(
            asked_out.at[step], asked.at[step], asked_sem.at[step]
        )

    for step in range(STEPS):
        ask(step).wait_recv()
        asked_copy(step).start()
    for step in range(STEPS):
        asked_copy(step).wait()
    for batch in range(batches):
        for i in range(LANES):
            row = asked[step_of(batch), half_of(batch) * LANES + i, 1]
            fwd[batch, i] = orb[row]
    for batch in range(batches):
        forward(batch).start()

    @pl.when(gz > 0)
    def _():
        rim_up().wait_recv()

    @pl.when(gz < slabs - 1)
    def _():
        rim_down().wait_recv()

    center = diel[...]
    tall = jnp.concatenate([rim[0], center, rim[1]], axis=0)
    wide[...] = jnp.zeros(wide.shape, wide.dtype)
    wide[:, 8 : 8 + nx, :] = center
    lane = lax.broadcasted_iota(jnp.int32, center.shape, 2)
    column = lax.broadcasted_iota(jnp.int32, center.shape, 1)
    level = lax.broadcasted_iota(jnp.int32, center.shape, 0) + gz * planes
    diagonal = screening * center
    made = []
    for axis_number in range(3):
        for offset in offsets:
            weight = near_weight if abs(offset) == 1 else far_weight
            if axis_number == 0:
                beyond = tall[2 + offset : 2 + offset + planes]
                place, length = level, slabs * planes
            elif axis_number == 1:
                beyond = wide[:, 8 + offset : 8 + offset + nx, :]
                place, length = column, nx
            else:
                beyond = pltpu.roll(center, (-offset) % ny, 2)
                place, length = lane, ny
            inside = (place + offset >= 0) & (place + offset < length)
            beyond = jnp.where(inside, beyond, 0.0)
            value = weight * 0.5 * (center + beyond)
            diagonal = diagonal + value
            made.append(jnp.where(inside, value, 0.0))
    reciprocal = 1.0 / diagonal
    rdiag[...] = reciprocal
    for number, value in enumerate(made):
        face[number] = (value * reciprocal).reshape(cells, ny)

    def send_up(batch, turn):
        return pltpu.make_async_remote_copy(
            src_ref=up_snd.at[batch, turn],
            dst_ref=lo_rcv.at[batch, turn],
            send_sem=up_s.at[batch, turn],
            recv_sem=lo_r.at[batch, turn],
            device_id=(me, gz + 1),
            device_id_type=MESH,
        )

    def send_down(batch, turn):
        return pltpu.make_async_remote_copy(
            src_ref=dn_snd.at[batch, turn],
            dst_ref=hi_rcv.at[batch, turn],
            send_sem=dn_s.at[batch, turn],
            recv_sem=hi_r.at[batch, turn],
            device_id=(me, gz - 1),
            device_id_type=MESH,
        )

    def publish(batch, turn, side):
        for z in range(2):
            for x in range(0, nx, 2):
                for source, target in ((planes, up_snd), (2, dn_snd)):
                    at = (source + z) * nx + x
                    both = jnp.concatenate(
                        [pot[batch, side, at], pot[batch, side, at + 1]], axis=0
                    )
                    target[batch, turn, z, x // 2] = both.astype(jnp.bfloat16)

        @pl.when(gz < slabs - 1)
        def _():
            send_up(batch, turn).start()

        @pl.when(gz > 0)
        def _():
            send_down(batch, turn).start()

    def begin(batch):
        forward(batch).wait_recv()
        step, half = step_of(batch), half_of(batch)
        live = count[0, step]
        for i in range(LANES):
            slot = half * LANES + i
            scale = jnp.where(slot < live, coupling, 0.0).astype(jnp.float32)
            first = orb[pairs[0, step, slot, 0]].astype(jnp.float32)
            second = sec[batch, i].astype(jnp.float32)
            value = (scale * (first * second)) * rdiag[...]
            nat[i * cells : (i + 1) * cells, :] = value.reshape(cells, ny)
        for cell in range(cells):
            value = nat[pl.ds(cell, LANES, stride=cells), :]
            base[batch, cell] = value
            pot[batch, 0, 2 * nx + cell] = value
        publish(batch, 0, 0)

    def unpack(source, batch, turn, side, start):
        for z in range(2):
            for x in range(0, nx, 2):
                both = source[batch, turn, z, x // 2].astype(jnp.float32)
                at = start + z * nx + x
                pot[batch, side, at] = both[:LANES]
                pot[batch, side, at + 1] = both[LANES:]

    def sweep(batch, turn):
        side = turn % 2

        @pl.when(gz > 0)
        def _():
            send_up(batch, turn).wait_recv()
            unpack(lo_rcv, batch, turn, side, 0)

        @pl.when(gz < slabs - 1)
        def _():
            send_down(batch, turn).wait_recv()
            unpack(hi_rcv, batch, turn, side, (planes + 2) * nx)

        def plane(z, carry):
            here = (z + 2) * nx
            row = z * nx
            line = [pot[batch, side, here + x] for x in range(nx)]
            for x in range(nx):
                total = base[batch, row + x]
                number = 0
                for axis_number in range(3):
                    for offset in offsets:
                        if axis_number == 0:
                            value = pot[batch, side, here + offset * nx + x]
                        elif axis_number == 1:
                            value = line[x + offset] if 0 <= x + offset < nx else None
                        else:
                            value = pltpu.roll(line[x], (-offset) % ny, 1)
                        if value is not None:
                            total = total + face[number, pl.ds(row + x, 1), :] * value
                        number += 1
                pot[batch, 1 - side, here + x] = total
            return carry

        lax.fori_loop(0, planes, plane, 0)

        @pl.when(turn < ROUNDS - 1)
        def _():
            publish(batch, turn + 1, 1 - side)

    def give_back(batch):
        return pltpu.make_async_remote_copy(
            src_ref=ret.at[batch],
            dst_ref=vis_out.at[batch],
            send_sem=ret_s.at[batch],
            recv_sem=ret_r.at[batch],
            device_id=(group(-step_of(batch) - 1), gz),
            device_id_type=MESH,
        )

    def keep(batch):
        return pltpu.make_async_copy(own.at[batch], own_out.at[batch], own_sem.at[batch])

    def finish(batch):
        step, half = step_of(batch), half_of(batch)
        side = ROUNDS % 2
        for cell in range(cells):
            nat[pl.ds(cell, LANES, stride=cells), :] = pot[batch, side, 2 * nx + cell]
        for i in range(LANES):
            slot = half * LANES + i
            value = nat[i * cells : (i + 1) * cells, :].reshape(planes, nx, ny)
            first = orb[pairs[0, step, slot, 0]].astype(jnp.float32)
            second = sec[batch, i].astype(jnp.float32)
            ret[batch, i] = value * first
            own[batch, i] = value * second
        give_back(batch).start()
        keep(batch).start()

    def diagonal_step(d, carry):
        def one(batch, inner):
            turn = d - batch

            @pl.when(turn == 0)
            def _():
                begin(batch)

            @pl.when((turn >= 1) & (turn <= ROUNDS))
            def _():
                sweep(batch, turn - 1)

            @pl.when(turn == ROUNDS)
            def _():
                finish(batch)

            return inner

        return lax.fori_loop(0, batches, one, carry)

    lax.fori_loop(0, ROUNDS + batches, diagonal_step, 0)

    for step in range(STEPS):
        ask(step).wait_send()

    @pl.when(gz < slabs - 1)
    def _():
        rim_up().wait_send()

    @pl.when(gz > 0)
    def _():
        rim_down().wait_send()

    def drain(number, carry):
        batch, turn = number // ROUNDS, number % ROUNDS

        @pl.when(gz < slabs - 1)
        def _():
            send_up(batch, turn).wait_send()

        @pl.when(gz > 0)
        def _():
            send_down(batch, turn).wait_send()

        return carry

    lax.fori_loop(0, batches * ROUNDS, drain, 0)
    for batch in range(batches):
        forward(batch).wait_send()
        keep(batch).wait()
        give_back(batch).wait()


def scatter_kernel(pairs, asked, own, vis, out):
    out[...] = jnp.zeros(out.shape, out.dtype)
    for batch in range(own.shape[0]):
        for i in range(LANES):
            slot = half_of(batch) * LANES + i
            row = pairs[0, step_of(batch), slot, 0]
            out[row] += own[batch, i]
            row = asked[step_of(batch), slot, 1]
            out[row] += vis[batch, i]


def per_device(groups, slabs, orbitals, dielectric, pairs, pair_count):
    rows, planes, nx, ny = orbitals.shape
    slots = pairs.shape[2]
    batches = STEPS * slots // LANES
    vmem = pl.BlockSpec(memory_space=pltpu.VMEM)
    smem = pl.BlockSpec(memory_space=pltpu.SMEM)
    anywhere = pl.BlockSpec(memory_space=pl.ANY)
    slab = (batches, LANES, planes, nx, ny)
    halo = (batches, ROUNDS, 2, nx // 2, 2 * LANES, ny)
    dma = pltpu.SemaphoreType.DMA
    own, vis, asked = pl.pallas_call(
        functools.partial(relax_kernel, groups, slabs),
        out_shape=(
            jax.ShapeDtypeStruct(slab, jnp.float32),
            jax.ShapeDtypeStruct(slab, jnp.float32),
            jax.ShapeDtypeStruct(pairs.shape[1:], jnp.int32),
        ),
        in_specs=[anywhere, vmem, smem, smem, anywhere],
        out_specs=(anywhere, anywhere, anywhere),
        scratch_shapes=[
            pltpu.VMEM(orbitals.shape, orbitals.dtype),
            pltpu.SMEM(pairs.shape[1:], jnp.int32),
            pltpu.VMEM((2, 2, nx, ny), jnp.float32),
            pltpu.VMEM((planes, nx + 16, ny), jnp.float32),
            pltpu.VMEM((12, planes * nx, ny), jnp.float32),
            pltpu.VMEM((planes, nx, ny), jnp.float32),
            pltpu.VMEM(slab, jnp.bfloat16),
            pltpu.VMEM(slab, jnp.bfloat16),
            pltpu.VMEM((LANES * planes * nx, ny), jnp.float32),
            pltpu.VMEM((batches, planes * nx, LANES, ny), jnp.float32),
            pltpu.VMEM((batches, 2, (planes + 4) * nx, LANES, ny), jnp.float32),
            pltpu.VMEM(halo, jnp.bfloat16),
            pltpu.VMEM(halo, jnp.bfloat16),
            pltpu.VMEM(halo, jnp.bfloat16),
            pltpu.VMEM(halo, jnp.bfloat16),
            pltpu.VMEM(slab, jnp.float32),
            pltpu.VMEM(slab, jnp.float32),
            dma,
            dma((STEPS,)),
            dma((STEPS,)),
            dma((STEPS,)),
            dma((2,)),
            dma((2,)),
            dma((batches,)),
            dma((batches,)),
            dma((batches, ROUNDS)),
            dma((batches, ROUNDS)),
            dma((batches, ROUNDS)),
            dma((batches, ROUNDS)),
            dma((batches,)),
            dma((batches,)),
            dma((batches,)),
        ],
        compiler_params=pltpu.CompilerParams(
            collective_id=0, has_side_effects=True, vmem_limit_bytes=48 << 20
        ),
        name="relax_pairs",
    )(orbitals, dielectric, pairs, pair_count, pairs)

    block = (batches, LANES, None, nx, ny)
    return pl.pallas_call(
        scatter_kernel,
        out_shape=jax.ShapeDtypeStruct(orbitals.shape, jnp.float32),
        grid_spec=pltpu.PrefetchScalarGridSpec(
            num_scalar_prefetch=2,
            grid=(planes,),
            in_specs=[
                pl.BlockSpec(block, lambda z, *_: (0, 0, z, 0, 0)),
                pl.BlockSpec(block, lambda z, *_: (0, 0, z, 0, 0)),
            ],
            out_specs=pl.BlockSpec((rows, None, nx, ny), lambda z, *_: (0, z, 0, 0)),
        ),
        name="add_by_row",
    )(pairs, asked, own, vis)


def solution(mesh):
    placed = (
        P("orb", "gz", None, None),
        P("gz", None, None),
        P("orb", None, None, None),
        P("orb", None),
    )
    return jax.shard_map(
        functools.partial(per_device, mesh.shape["orb"], mesh.shape["gz"]),
        mesh=mesh,
        in_specs=placed,
        out_specs=P("orb", "gz", None, None),
        check_vma=False,
    )
```

time: 136 us -> 91.5 us (0.67); the launches traced: 133 us -> 91.1 us
  Pallas kernels: 0 us -> 84.8 us
  starting transfers between devices: 58.1 us -> 0 us
  waiting for transfers between devices: 43.9 us -> 0 us
  other arithmetic: 22.9 us -> 0 us
  local copies, waits for them, and re-layouts: 7.92 us -> 6.36 us
    pallas_call x0 -> x2, Pallas kernels: none -> 84.8 us  [the longest x1 79.1 us: per_device(): pl.pallas_call(functools.partial(relax_kernel, groups, slabs), out_shape=...]
    ppermute x18 -> x0, starting transfers between devices: 58.1 us -> none  [the longest x6 37.8 us: with_halo(): after = lax.ppermute(leading, axis, down)]
    ppermute x18 -> x0, waiting for transfers between devices: 43.9 us -> none  [the longest x6 20.5 us: with_halo(): before = lax.ppermute(last, axis, up)]
    scatter-add x3 -> x0, other arithmetic: 10.8 us -> none  [the longest x2 5.99 us: per_device(): exchange = exchange.at[wanted[step - 1]].add(part)]
    convert_element_type x10 -> x0, other arithmetic: 8.17 us -> none  [the longest x5 7.42 us: per_device(): potential.astype(jnp.bfloat16)]
    unnamed x8 -> x15, local copies, waits for them, and re-layouts: 0.02 us -> 6.36 us
    slice x8 -> x0, local copies, waits for them, and re-layouts: 2.66 us -> none  [the longest x1 1.08 us: per_device(): part = cycle(back[(step - 1) * slots:step * slots], 'orb', -step)]
    mul x3 -> x0, other arithmetic: 2.55 us -> none  [the longest x1 2.26 us: per_device(): back = potential * first]
  transfers between devices with their start and end apart: 18 -> 0, of which waited for: 15 -> 0; matrix products, arithmetic and copies ran while one was open for 11% -> 0% of each run, Pallas kernels for 0% -> 0%
where the time goes in v2:
time: 91.5 us; the launch traced here: 91.1 us
  Pallas kernels  84.8 us (93%)
  local copies, waits for them, and re-layouts  6.36 us (7%)
    pallas_call x1, Pallas kernels, per_device(): pl.pallas_call(functools.partial(relax_kernel, groups, slabs), out_shape=...  79.1 us
    unnamed x15, local copies, waits for them, and re-layouts  6.36 us
    pallas_call x1, Pallas kernels, per_device(): pl.pallas_call(scatter_kernel, out_shape=jax.ShapeDtypeStruct(orbitals.sh...  5.68 us

profile of v2, /device:TPU:2, one launch (start us, length us, event | category | flops | bytes accessed | tf_op | source)
XLA Modules:
  0.0 91.1 jit_solution(14706376157294850099)
XLA Ops:
  0.0 0.8 copy.7.pairs.pairs_hbm
  0.8 0.0 copy-start
  0.8 1.6 %copy-done = bf16[128,4,16,128]{3,2,1,0:T(8,128)(2,1)S(1)} copy-done((bf16[128,4,16,128]{3,2,1,0:T(8,128)(2,1)S(1)}, bf16[128,4,16,128]{3,2,1,0:T(8,128)(2,1)}, u32[]{:S(2)}) %copy-start) | copy-done | bytes 2097176
  2.4 0.0 copy-start.4
  2.4 0.8 copy-done.4
  3.1 0.0 copy-start.6
  3.1 0.7 copy-done.6
  3.8 0.0 copy-start.3
  3.8 79.1 %relax_pairs.1 = (f32[4,8,4,16,128]{4,3,2,1,0:T(8,128)S(1)}, f32[4,8,4,16,128]{4,3,2,1,0:T(8,128)S(1)}, s32[2,16,2]{2,1,0:T(8,128)S(1)}) custom-call(bf16[128,4,16,128]{3,2,1,0:T(8,128)(2,1)S(1)} %copy-done, f32[4,16,128]{2,1,0:T(8,128)S(1)} %copy-done.4, s32[1,2,16,2]{3,2,1,0:T(8,128)S(1)} %copy.7.pairs.pairs_hbm, s32[1,2]{1,0:T(1,128)S(1)} %copy-done.6, ...), custom_call_target="tpu_custom_call" | custom-call | tf_op jit(solution)/shard_map/relax_pairs/pallas_call | solution.py:436
  82.9 0.0 copy-start.1
  82.9 1.0 %copy-done.1 = f32[4,8,4,16,128]{4,3,2,1,0:T(8,128)} copy-done((f32[4,8,4,16,128]{4,3,2,1,0:T(8,128)}, f32[4,8,4,16,128]{4,3,2,1,0:T(8,128)S(1)}, u32[]{:S(2)}) %copy-start.1) | copy-done | bytes 1048600
  83.8 0.0 copy-start.2
  83.8 1.0 %copy-done.2 = f32[4,8,4,16,128]{4,3,2,1,0:T(8,128)} copy-done((f32[4,8,4,16,128]{4,3,2,1,0:T(8,128)}, f32[4,8,4,16,128]{4,3,2,1,0:T(8,128)S(1)}, u32[]{:S(2)}) %copy-start.2) | copy-done | bytes 1048600
  84.9 0.0 copy-start.5
  84.9 0.6 copy-done.5
  85.5 0.0 copy-done.3
  85.5 5.7 %add_by_row.1 = f32[128,4,16,128]{3,2,1,0:T(8,128)} custom-call(s32[1,2,16,2]{3,2,1,0:T(8,128)} %copy-done.3, s32[2,16,2]{2,1,0:T(8,128)} %copy-done.5, f32[4,8,4,16,128]{4,3,2,1,0:T(8,128)} %copy-done.1, f32[4,8,4,16,128]{4,3,2,1,0:T(8,128)} %copy-done.2), custom_call_target="tpu_custom_call" | custom-call | tf_op jit(solution)/shard_map/add_by_row/pallas_call | solution.py:486
Async XLA Ops:
  0.8 1.6 %copy-start = (bf16[128,4,16,128]{3,2,1,0:T(8,128)(2,1)S(1)}, bf16[128,4,16,128]{3,2,1,0:T(8,128)(2,1)}, u32[]{:S(2)}) copy-start(bf16[128,4,16,128]{3,2,1,0:T(8,128)(2,1)} %orb_hbm.1) | copy-start | bytes 6291460
  2.4 0.8 copy-start.4
  3.1 0.7 copy-start.6
  3.8 81.7 %copy-start.3 = (s32[1,2,16,2]{3,2,1,0:T(8,128)}, s32[1,2,16,2]{3,2,1,0:T(8,128)S(1)}, u32[]{:S(2)}) copy-start(s32[1,2,16,2]{3,2,1,0:T(8,128)S(1)} %copy.7.pairs.pairs_hbm) | copy-start | bytes 772
  82.9 1.0 %copy-start.1 = (f32[4,8,4,16,128]{4,3,2,1,0:T(8,128)}, f32[4,8,4,16,128]{4,3,2,1,0:T(8,128)S(1)}, u32[]{:S(2)}) copy-start(f32[4,8,4,16,128]{4,3,2,1,0:T(8,128)S(1)} %get-tuple-element.9.own) | copy-start | bytes 3145732
  83.8 1.0 %copy-start.2 = (f32[4,8,4,16,128]{4,3,2,1,0:T(8,128)}, f32[4,8,4,16,128]{4,3,2,1,0:T(8,128)S(1)}, u32[]{:S(2)}) copy-start(f32[4,8,4,16,128]{4,3,2,1,0:T(8,128)S(1)} %get-tuple-element.10.vis) | copy-start | bytes 3145732
  84.9 0.6 copy-start.5

commit v3 on v2

v3 whole, which is shorter than its diff:
```python
import functools
import math

import jax
import jax.numpy as jnp
from jax import lax
from jax.experimental import pallas as pl
from jax.experimental.pallas import tpu as pltpu
from jax.sharding import PartitionSpec as P

SWEEPS = 6
STEPS = 2
ROUNDS = SWEEPS - 1
LANES = 8

near_weight = 1.0
far_weight = 0.25
screening = 0.02
coupling = 4.0 * math.pi
offsets = (-2, -1, 1, 2)
MESH = pl.DeviceIdType.MESH


PUSHED = 2


def step_of(batch):
    return 1 if batch < PUSHED else 0


def half_of(batch):
    return batch % 2


def relax_kernel(
    groups,
    slabs,
    orb_hbm,
    diel_hbm,
    pairs_hbm,
    count_hbm,
    own,
    vis,
    asked,
    orb,
    diel,
    pairs,
    count,
    rim,
    wide,
    face,
    rdiag,
    fwd,
    sec,
    nat,
    base,
    pot,
    snd,
    rcv,
    ret,
    load_sem,
    ask_s,
    ask_r,
    rim_s,
    rim_r,
    fwd_s,
    fwd_r,
    up_s,
    up_r,
    dn_s,
    dn_r,
    ret_s,
    ret_r,
):
    me = lax.axis_index("orb")
    gz = lax.axis_index("gz")
    planes, nx, ny = diel.shape
    batches = sec.shape[0]
    cells = planes * nx

    def group(distance):
        return lax.rem(me + distance + groups, groups)

    barrier = pltpu.get_barrier_semaphore()
    for distance in (-2, -1, 1, 2):
        pl.semaphore_signal(
            barrier, inc=1, device_id=(group(distance), gz), device_id_type=MESH
        )

    @pl.when(gz > 0)
    def _():
        pl.semaphore_signal(barrier, inc=1, device_id=(me, gz - 1), device_id_type=MESH)

    @pl.when(gz < slabs - 1)
    def _():
        pl.semaphore_signal(barrier, inc=1, device_id=(me, gz + 1), device_id_type=MESH)

    loads = [
        pltpu.make_async_copy(source, target, load_sem.at[number])
        for number, (source, target) in enumerate(
            ((pairs_hbm, pairs), (count_hbm, count), (orb_hbm, orb), (diel_hbm, diel))
        )
    ]
    for load in loads:
        load.start()

    @pl.when(gz == 0)
    def _():
        rim[0] = jnp.zeros(rim.shape[1:], rim.dtype)
        pot[:, :, 0 : 2 * nx] = jnp.zeros((batches, 2, 2 * nx, LANES, ny), jnp.float32)

    @pl.when(gz == slabs - 1)
    def _():
        rim[1] = jnp.zeros(rim.shape[1:], rim.dtype)
        pot[:, :, (planes + 2) * nx :] = jnp.zeros(
            (batches, 2, 2 * nx, LANES, ny), jnp.float32
        )

    for load in loads:
        load.wait()

    for batch in range(PUSHED):
        step = step_of(batch)
        live = count[0, step]
        for i in range(LANES):
            slot = half_of(batch) * LANES + i
            value = orb[pairs[0, step, 0, slot]].astype(jnp.float32)
            keep = jnp.where(slot < live, 1.0, 0.0).astype(jnp.float32)
            fwd[batch, i] = (value * keep).astype(jnp.bfloat16)

    @pl.when((gz == 0) | (gz == slabs - 1))
    def _():
        pl.semaphore_wait(barrier, 5)

    @pl.when((gz > 0) & (gz < slabs - 1))
    def _():
        pl.semaphore_wait(barrier, 6)

    def ask(step):
        return pltpu.make_async_remote_copy(
            src_ref=pairs.at[0, step],
            dst_ref=asked.at[step],
            send_sem=ask_s.at[step],
            recv_sem=ask_r.at[step],
            device_id=(group(-step - 1), gz),
            device_id_type=MESH,
        )

    for step in range(STEPS):
        ask(step).start()

    def forward(batch):
        target = -step_of(batch) - 1 if batch < PUSHED else step_of(batch) + 1
        return pltpu.make_async_remote_copy(
            src_ref=fwd.at[batch],
            dst_ref=sec.at[batch],
            send_sem=fwd_s.at[batch],
            recv_sem=fwd_r.at[batch],
            device_id=(group(target), gz),
            device_id_type=MESH,
        )

    for batch in range(PUSHED):
        forward(batch).start()

    def rim_up():
        return pltpu.make_async_remote_copy(
            src_ref=diel.at[pl.ds(planes - 2, 2)],
            dst_ref=rim.at[0],
            send_sem=rim_s.at[0],
            recv_sem=rim_r.at[0],
            device_id=(me, gz + 1),
            device_id_type=MESH,
        )

    def rim_down():
        return pltpu.make_async_remote_copy(
            src_ref=diel.at[pl.ds(0, 2)],
            dst_ref=rim.at[1],
            send_sem=rim_s.at[1],
            recv_sem=rim_r.at[1],
            device_id=(me, gz - 1),
            device_id_type=MESH,
        )

    @pl.when(gz < slabs - 1)
    def _():
        rim_up().start()

    @pl.when(gz > 0)
    def _():
        rim_down().start()

    for step in range(STEPS):
        ask(step).wait_recv()
    for batch in range(PUSHED, batches):
        for i in range(LANES):
            slot = half_of(batch) * LANES + i
            fwd[batch, i] = orb[asked[step_of(batch), 1, slot]]
    for batch in range(PUSHED, batches):
        forward(batch).start()

    @pl.when(gz > 0)
    def _():
        rim_up().wait_recv()

    @pl.when(gz < slabs - 1)
    def _():
        rim_down().wait_recv()

    center = diel[...]
    tall = jnp.concatenate([rim[0], center, rim[1]], axis=0)
    wide[...] = jnp.zeros(wide.shape, wide.dtype)
    wide[:, 8 : 8 + nx, :] = center
    lane = lax.broadcasted_iota(jnp.int32, center.shape, 2)
    column = lax.broadcasted_iota(jnp.int32, center.shape, 1)
    level = lax.broadcasted_iota(jnp.int32, center.shape, 0) + gz * planes
    diagonal = screening * center
    made = []
    for axis_number in range(3):
        for offset in offsets:
            weight = near_weight if abs(offset) == 1 else far_weight
            if axis_number == 0:
                beyond = tall[2 + offset : 2 + offset + planes]
                place, length = level, slabs * planes
            elif axis_number == 1:
                beyond = wide[:, 8 + offset : 8 + offset + nx, :]
                place, length = column, nx
            else:
                beyond = pltpu.roll(center, (-offset) % ny, 2)
                place, length = lane, ny
            inside = (place + offset >= 0) & (place + offset < length)
            beyond = jnp.where(inside, beyond, 0.0)
            value = weight * 0.5 * (center + beyond)
            diagonal = diagonal + value
            made.append(jnp.where(inside, value, 0.0))
    reciprocal = 1.0 / diagonal
    rdiag[...] = reciprocal
    for number, value in enumerate(made):
        face[number] = (value * reciprocal).reshape(cells, ny)

    def send_up(batch, turn):
        return pltpu.make_async_remote_copy(
            src_ref=snd.at[batch, turn, 1],
            dst_ref=rcv.at[batch, turn, 0],
            send_sem=up_s.at[batch, turn],
            recv_sem=up_r.at[batch, turn],
            device_id=(me, gz + 1),
            device_id_type=MESH,
        )

    def send_down(batch, turn):
        return pltpu.make_async_remote_copy(
            src_ref=snd.at[batch, turn, 0],
            dst_ref=rcv.at[batch, turn, 1],
            send_sem=dn_s.at[batch, turn],
            recv_sem=dn_r.at[batch, turn],
            device_id=(me, gz - 1),
            device_id_type=MESH,
        )

    def publish(batch, turn):
        @pl.when(gz < slabs - 1)
        def _():
            send_up(batch, turn).start()

        @pl.when(gz > 0)
        def _():
            send_down(batch, turn).start()

    def pack(batch, turn, z, line):
        for x in range(0, nx, 2):
            both = jnp.concatenate([line[x], line[x + 1]], axis=0)
            snd[batch, turn, z // 2, z % 2, x // 2] = both.astype(jnp.bfloat16)

    def local_row(batch, i):
        slot = half_of(batch) * LANES + i
        if batch < PUSHED:
            return orb[asked[step_of(batch), 1, slot]].astype(jnp.float32)
        return orb[pairs[0, step_of(batch), 0, slot]].astype(jnp.float32)

    def begin(batch):
        forward(batch).wait_recv()
        live = count[0, step_of(batch)]
        for i in range(LANES):
            slot = half_of(batch) * LANES + i
            scale = coupling
            if batch >= PUSHED:
                scale = jnp.where(slot < live, coupling, 0.0).astype(jnp.float32)
            other = sec[batch, i].astype(jnp.float32)
            value = (scale * (local_row(batch, i) * other)) * rdiag[...]
            nat[batch, i * cells : (i + 1) * cells, :] = value.reshape(cells, ny)
        for z in range(planes):
            line = [
                nat[batch, pl.ds(z * nx + x, LANES, stride=cells), :] for x in range(nx)
            ]
            for x in range(nx):
                base[batch, z * nx + x] = line[x]
                pot[batch, 0, (2 + z) * nx + x] = line[x]
            pack(batch, 0, z, line)
        publish(batch, 0)

    def unpack(batch, turn, side, edge, start):
        for z in range(2):
            for x in range(0, nx, 2):
                both = rcv[batch, turn, edge, z, x // 2].astype(jnp.float32)
                at = start + z * nx + x
                pot[batch, side, at] = both[:LANES]
                pot[batch, side, at + 1] = both[LANES:]

    def sweep(batch, turn, last):
        side = turn % 2

        @pl.when(gz > 0)
        def _():
            send_up(batch, turn).wait_recv()
            unpack(batch, turn, side, 0, 0)

        @pl.when(gz < slabs - 1)
        def _():
            send_down(batch, turn).wait_recv()
            unpack(batch, turn, side, 1, (planes + 2) * nx)

        def plane(z, carry):
            here = (z + 2) * nx
            row = z * nx
            line = [pot[batch, side, here + x] for x in range(nx)]
            totals = []
            for x in range(nx):
                number = 0
                parts = []
                for axis_number in range(3):
                    part = None
                    for offset in offsets:
                        if axis_number == 0:
                            value = pot[batch, side, here + offset * nx + x]
                        elif axis_number == 1:
                            value = line[x + offset] if 0 <= x + offset < nx else None
                        else:
                            value = pltpu.roll(line[x], (-offset) % ny, 1)
                        if value is not None:
                            value = face[number, pl.ds(row + x, 1), :] * value
                            part = value if part is None else part + value
                        number += 1
                    parts.append(part)
                totals.append((base[batch, row + x] + parts[0]) + (parts[1] + parts[2]))
            for x in range(nx):
                pot[batch, 1 - side, here + x] = totals[x]
            if not last:
                pack(batch, turn + 1, z, totals)
            return carry

        lax.fori_loop(0, planes, plane, 0)
        if not last:
            publish(batch, turn + 1)

    def give_back(batch):
        target = step_of(batch) + 1 if batch < PUSHED else -step_of(batch) - 1
        return pltpu.make_async_remote_copy(
            src_ref=ret.at[batch],
            dst_ref=vis.at[batch],
            send_sem=ret_s.at[batch],
            recv_sem=ret_r.at[batch],
            device_id=(group(target), gz),
            device_id_type=MESH,
        )

    def finish(batch):
        side = ROUNDS % 2
        for cell in range(cells):
            nat[batch, pl.ds(cell, LANES, stride=cells), :] = pot[
                batch, side, 2 * nx + cell
            ]
        values = [
            nat[batch, i * cells : (i + 1) * cells, :].reshape(planes, nx, ny)
            for i in range(LANES)
        ]
        for i in range(LANES):
            ret[batch, i] = values[i] * local_row(batch, i)
        give_back(batch).start()
        for i in range(LANES):
            own[batch, i] = values[i] * sec[batch, i].astype(jnp.float32)

    for batch in range(batches):
        begin(batch)

    def turns(turn, carry):
        def one(batch, inner):
            sweep(batch, turn, False)
            return inner

        return lax.fori_loop(0, batches, one, carry)

    lax.fori_loop(0, ROUNDS - 1, turns, 0)
    for batch in range(batches):
        sweep(batch, ROUNDS - 1, True)
        finish(batch)

    for step in range(STEPS):
        ask(step).wait_send()

    @pl.when(gz < slabs - 1)
    def _():
        rim_up().wait_send()

    @pl.when(gz > 0)
    def _():
        rim_down().wait_send()

    def drain(number, carry):
        batch, turn = number // ROUNDS, number % ROUNDS

        @pl.when(gz < slabs - 1)
        def _():
            send_up(batch, turn).wait_send()

        @pl.when(gz > 0)
        def _():
            send_down(batch, turn).wait_send()

        return carry

    lax.fori_loop(0, batches * ROUNDS, drain, 0)
    for batch in range(batches):
        forward(batch).wait_send()
        give_back(batch).wait()


def scatter_kernel(pairs, asked, own, vis, out, acc, sem):
    planes = acc.shape[1]
    half = planes // 2
    copies = []
    for part in range(2):
        where = pl.ds(part * half, half)
        acc[:, where] = jnp.zeros((acc.shape[0], half) + acc.shape[2:], acc.dtype)
        for batch in range(own.shape[0]):
            step = step_of(batch)
            for i in range(LANES):
                slot = half_of(batch) * LANES + i
                mine, theirs = pairs[0, step, 0, slot], asked[step, 1, slot]
                kept, returned = (theirs, mine) if batch < PUSHED else (mine, theirs)
                acc[kept, where] += own[batch, i, where]
                acc[returned, where] += vis[batch, i, where]
        copy = pltpu.make_async_copy(acc.at[:, where], out.at[:, where], sem.at[part])
        copy.start()
        copies.append(copy)
    for copy in copies:
        copy.wait()


def per_device(groups, slabs, orbitals, dielectric, pairs, pair_count):
    rows, planes, nx, ny = orbitals.shape
    pairs = jnp.swapaxes(pairs, 2, 3)
    slots = pairs.shape[3]
    batches = STEPS * slots // LANES
    vmem = pl.BlockSpec(memory_space=pltpu.VMEM)
    smem = pl.BlockSpec(memory_space=pltpu.SMEM)
    hbm = pl.BlockSpec(memory_space=pltpu.HBM)
    slab = (batches, LANES, planes, nx, ny)
    halo = (batches, ROUNDS, 2, 2, nx // 2, 2 * LANES, ny)
    dma = pltpu.SemaphoreType.DMA
    own, vis, asked = pl.pallas_call(
        functools.partial(relax_kernel, groups, slabs),
        out_shape=(
            jax.ShapeDtypeStruct(slab, jnp.float32),
            jax.ShapeDtypeStruct(slab, jnp.float32),
            jax.ShapeDtypeStruct(pairs.shape[1:], jnp.int32),
        ),
        in_specs=[hbm, hbm, hbm, hbm],
        out_specs=(vmem, vmem, smem),
        scratch_shapes=[
            pltpu.VMEM(orbitals.shape, orbitals.dtype),
            pltpu.VMEM(dielectric.shape, jnp.float32),
            pltpu.SMEM(pairs.shape, jnp.int32),
            pltpu.SMEM(pair_count.shape, jnp.int32),
            pltpu.VMEM((2, 2, nx, ny), jnp.float32),
            pltpu.VMEM((planes, nx + 16, ny), jnp.float32),
            pltpu.VMEM((12, planes * nx, ny), jnp.float32),
            pltpu.VMEM((planes, nx, ny), jnp.float32),
            pltpu.VMEM(slab, jnp.bfloat16),
            pltpu.VMEM(slab, jnp.bfloat16),
            pltpu.VMEM((batches, LANES * planes * nx, ny), jnp.float32),
            pltpu.VMEM((batches, planes * nx, LANES, ny), jnp.float32),
            pltpu.VMEM((batches, 2, (planes + 4) * nx, LANES, ny), jnp.float32),
            pltpu.VMEM(halo, jnp.bfloat16),
            pltpu.VMEM(halo, jnp.bfloat16),
            pltpu.VMEM(slab, jnp.float32),
            dma((4,)),
            dma((STEPS,)),
            dma((STEPS,)),
            dma((2,)),
            dma((2,)),
            dma((batches,)),
            dma((batches,)),
            dma((batches, ROUNDS)),
            dma((batches, ROUNDS)),
            dma((batches, ROUNDS)),
            dma((batches, ROUNDS)),
            dma((batches,)),
            dma((batches,)),
        ],
        compiler_params=pltpu.CompilerParams(
            collective_id=0, has_side_effects=True, vmem_limit_bytes=48 << 20
        ),
        name="relax_pairs",
    )(orbitals, dielectric, pairs, pair_count)

    return pl.pallas_call(
        scatter_kernel,
        out_shape=jax.ShapeDtypeStruct(orbitals.shape, jnp.float32),
        in_specs=[smem, smem, vmem, vmem],
        out_specs=hbm,
        scratch_shapes=[pltpu.VMEM(orbitals.shape, jnp.float32), dma((2,))],
        compiler_params=pltpu.CompilerParams(vmem_limit_bytes=32 << 20),
        name="add_by_row",
    )(pairs, asked, own, vis)


def solution(mesh):
    placed = (
        P("orb", "gz", None, None),
        P("gz", None, None),
        P("orb", None, None, None),
        P("orb", None),
    )
    return jax.shard_map(
        functools.partial(per_device, mesh.shape["orb"], mesh.shape["gz"]),
        mesh=mesh,
        in_specs=placed,
        out_specs=P("orb", "gz", None, None),
        check_vma=False,
    )
```

time: 91.5 us -> 72.8 us (0.80)
  Pallas kernels: 84.8 us -> 68.9 us
  local copies, waits for them, and re-layouts: 6.36 us -> 3.68 us
    pallas_call x1, Pallas kernels: 79.1 us -> 65.9 us  [per_device(): pl.pallas_call(functools.partial(relax_kernel, groups, slabs), out_shape=...]
    unnamed x15 -> x8, local copies, waits for them, and re-layouts: 6.36 us -> 3.68 us
    pallas_call x1, Pallas kernels: 5.68 us -> 3.08 us  [per_device(): pl.pallas_call(scatter_kernel, out_shape=jax.ShapeDtypeStruct(orbitals.sh...]
where the time goes in v3:
time: 72.8 us; the launch traced here: 72.6 us
  Pallas kernels  68.9 us (95%)
  local copies, waits for them, and re-layouts  3.68 us (5%)
    pallas_call x1, Pallas kernels, per_device(): pl.pallas_call(functools.partial(relax_kernel, groups, slabs), out_shape=...  65.9 us
    unnamed x8, local copies, waits for them, and re-layouts  3.68 us
    pallas_call x1, Pallas kernels, per_device(): pl.pallas_call(scatter_kernel, out_shape=jax.ShapeDtypeStruct(orbitals.sh...  3.08 us

profile of v3, /device:TPU:2, one launch (start us, length us, event | category | flops | bytes accessed | tf_op | source)
XLA Modules:
  0.0 72.6 jit_solution(4423368541459265676)
XLA Ops:
  0.0 0.0 copy-start
  0.0 1.6 %copy-done = bf16[128,4,16,128]{3,2,1,0:T(8,128)(2,1)S(1)} copy-done((bf16[128,4,16,128]{3,2,1,0:T(8,128)(2,1)S(1)}, bf16[128,4,16,128]{3,2,1,0:T(8,128)(2,1)}, u32[]{:S(2)}) %copy-start) | copy-done | bytes 2097176
  1.6 0.0 copy-start.1
  1.6 0.8 %copy-done.1 = f32[4,16,128]{2,1,0:T(8,128)S(1)} copy-done((f32[4,16,128]{2,1,0:T(8,128)S(1)}, f32[4,16,128]{2,1,0:T(8,128)}, u32[]{:S(2)}) %copy-start.1) | copy-done | bytes 32792
  2.4 0.0 copy-start.2
  2.4 0.7 copy-done.2
  3.0 0.0 copy-start.3
  3.0 0.7 copy-done.3
  3.7 65.9 %relax_pairs.1 = (f32[4,8,4,16,128]{4,3,2,1,0:T(8,128)S(1)}, f32[4,8,4,16,128]{4,3,2,1,0:T(8,128)S(1)}, s32[2,2,16]{2,1,0:T(2,128)S(1)}) custom-call(bf16[128,4,16,128]{3,2,1,0:T(8,128)(2,1)S(1)} %copy-done, f32[4,16,128]{2,1,0:T(8,128)S(1)} %copy-done.1, s32[1,2,2,16]{3,2,1,0:T(2,128)S(1)} %bitcast.1, s32[1,2]{1,0:T(1,128)S(1)} %copy-done.3), custom_call_target="tpu_custom_call" | custom-call | tf_op jit(solution)/shard_map/relax_pairs/pallas_call | solution.py:462
  69.6 3.1 %add_by_row.1 = f32[128,4,16,128]{3,2,1,0:T(8,128)} custom-call(s32[1,2,2,16]{3,2,1,0:T(2,128)S(1)} %bitcast.2, s32[2,2,16]{2,1,0:T(2,128)S(1)} %get-tuple-element.8.asked, f32[4,8,4,16,128]{4,3,2,1,0:T(8,128)S(1)} %get-tuple-element.9.own, f32[4,8,4,16,128]{4,3,2,1,0:T(8,128)S(1)} %get-tuple-element.10.vis), custom_call_target="tpu_custom_call" | custom-call | tf_op jit(solution)/shard_map/add_by_row/pallas_call | solution.py:508
Async XLA Ops:
  0.0 1.6 %copy-start = (bf16[128,4,16,128]{3,2,1,0:T(8,128)(2,1)S(1)}, bf16[128,4,16,128]{3,2,1,0:T(8,128)(2,1)}, u32[]{:S(2)}) copy-start(bf16[128,4,16,128]{3,2,1,0:T(8,128)(2,1)} %orb_hbm.1) | copy-start | bytes 6291460
  1.6 0.8 %copy-start.1 = (f32[4,16,128]{2,1,0:T(8,128)S(1)}, f32[4,16,128]{2,1,0:T(8,128)}, u32[]{:S(2)}) copy-start(f32[4,16,128]{2,1,0:T(8,128)} %diel_hbm.1) | copy-start | bytes 98308
  2.4 0.7 copy-start.2
  3.0 0.7 copy-start.3

commit v4 on v3

--- a/solution.py
+++ b/solution.py
@@ -25,11 +25,11 @@
 
 
 def step_of(batch):
-    return 1 if batch < PUSHED else 0
+    return 1 - batch % 2
 
 
 def half_of(batch):
-    return batch % 2
+    return batch // 2
 
 
 def relax_kernel(
@@ -385,14 +385,15 @@
         begin(batch)
 
     def turns(turn, carry):
-        def one(batch, inner):
+        def one(number, inner):
+            batch = jnp.where(turn == 0, number, (number % 2) * 2 + number // 2)
             sweep(batch, turn, False)
             return inner
 
         return lax.fori_loop(0, batches, one, carry)
 
     lax.fori_loop(0, ROUNDS - 1, turns, 0)
-    for batch in range(batches):
+    for batch in (0, 2, 1, 3):
         sweep(batch, ROUNDS - 1, True)
         finish(batch)
 
@@ -452,6 +453,10 @@
     rows, planes, nx, ny = orbitals.shape
     pairs = jnp.swapaxes(pairs, 2, 3)
     slots = pairs.shape[3]
+    orbitals, dielectric, pairs, pair_count = (
+        pltpu.with_memory_space_constraint(array, pltpu.HBM)
+        for array in (orbitals, dielectric, pairs, pair_count)
+    )
     batches = STEPS * slots // LANES
     vmem = pl.BlockSpec(memory_space=pltpu.VMEM)
     smem = pl.BlockSpec(memory_space=pltpu.SMEM)

time: 72.8 us -> 68 us (0.934)
  local copies, waits for them, and re-layouts: 3.68 us -> 0 us
  Pallas kernels: 68.9 us -> 67.9 us
    unnamed x8 -> x0, local copies, waits for them, and re-layouts: 3.68 us -> none
    pallas_call x1, Pallas kernels: 65.9 us -> 64.7 us  [per_device(): pl.pallas_call(functools.partial(relax_kernel, groups, slabs), out_shape=...]
where the time goes in v4:
time: 68 us; the launch traced here: 67.9 us
  Pallas kernels  67.9 us (100%)
    pallas_call x1, Pallas kernels, per_device(): pl.pallas_call(functools.partial(relax_kernel, groups, slabs), out_shape=...  64.7 us
    pallas_call x1, Pallas kernels, per_device(): pl.pallas_call(scatter_kernel, out_shape=jax.ShapeDtypeStruct(orbitals.sh...  3.18 us

profile of v4, /device:TPU:2, one launch (start us, length us, event | category | flops | bytes accessed | tf_op | source)
XLA Modules:
  0.0 67.9 jit_solution(7773706837382754326)
XLA Ops:
  0.0 64.7 %relax_pairs.1 = (f32[4,8,4,16,128]{4,3,2,1,0:T(8,128)S(1)}, f32[4,8,4,16,128]{4,3,2,1,0:T(8,128)S(1)}, s32[2,2,16]{2,1,0:T(2,128)S(1)}) custom-call(bf16[128,4,16,128]{3,2,1,0:T(8,128)(2,1)} %orb_hbm.1, f32[4,16,128]{2,1,0:T(8,128)} %diel_hbm.1, s32[1,2,2,16]{3,2,1,0:T(2,128)} %bitcast.1, s32[1,2]{1,0:T(1,128)} %count_hbm.1), custom_call_target="tpu_custom_call" | custom-call | tf_op jit(solution)/shard_map/relax_pairs/pallas_call | solution.py:467
  64.7 3.2 %add_by_row.1 = f32[128,4,16,128]{3,2,1,0:T(8,128)} custom-call(s32[1,2,2,16]{3,2,1,0:T(2,128)} %bitcast.2, s32[2,2,16]{2,1,0:T(2,128)S(1)} %get-tuple-element.8.asked, f32[4,8,4,16,128]{4,3,2,1,0:T(8,128)S(1)} %get-tuple-element.9.own, f32[4,8,4,16,128]{4,3,2,1,0:T(8,128)S(1)} %get-tuple-element.10.vis), custom_call_target="tpu_custom_call" | custom-call | tf_op jit(solution)/shard_map/add_by_row/pallas_call | solution.py:513

commit v5 on v4

--- a/solution.py
+++ b/solution.py
@@ -78,6 +78,8 @@
     batches = sec.shape[0]
     cells = planes * nx
 
+    far = (me // 2) % (groups // 4) == groups // 4 - 1
+
     def group(distance):
         return lax.rem(me + distance + groups, groups)
 
@@ -377,25 +379,53 @@
         ]
         for i in range(LANES):
             ret[batch, i] = values[i] * local_row(batch, i)
-        give_back(batch).start()
+        if batch < PUSHED:
+
+            @pl.when(jnp.logical_not(far))
+            def _():
+                give_back(batch).start()
+
+        else:
+            give_back(batch).start()
         for i in range(LANES):
             own[batch, i] = values[i] * sec[batch, i].astype(jnp.float32)
 
-    for batch in range(batches):
+    for batch in range(PUSHED):
         begin(batch)
 
+    def early(batch, carry):
+        sweep(batch, 0, False)
+        return carry
+
+    lax.fori_loop(0, PUSHED, early, 0)
+    for batch in range(PUSHED, batches):
+        begin(batch)
+
     def turns(turn, carry):
-        def one(number, inner):
-            batch = jnp.where(turn == 0, number, (number % 2) * 2 + number // 2)
-            sweep(batch, turn, False)
+        def one(batch, inner):
+            sweep(batch, turn + 1 - batch // PUSHED, False)
             return inner
 
         return lax.fori_loop(0, batches, one, carry)
 
-    lax.fori_loop(0, ROUNDS - 1, turns, 0)
-    for batch in (0, 2, 1, 3):
+    lax.fori_loop(0, ROUNDS - 2, turns, 0)
+    for batch in range(PUSHED):
         sweep(batch, ROUNDS - 1, True)
         finish(batch)
+
+    def late(batch, carry):
+        sweep(batch, ROUNDS - 2, False)
+        return carry
+
+    lax.fori_loop(PUSHED, batches, late, 0)
+    for batch in range(PUSHED, batches):
+        sweep(batch, ROUNDS - 1, True)
+        finish(batch)
+
+    @pl.when(far)
+    def _():
+        for batch in range(PUSHED):
+            give_back(batch).start()
 
     for step in range(STEPS):
         ask(step).wait_send()

time: 68 us -> 66.9 us (0.984)
  Pallas kernels: 67.9 us -> 66.8 us
    pallas_call x1, Pallas kernels: 64.7 us -> 63.6 us  [per_device(): pl.pallas_call(functools.partial(relax_kernel, groups, slabs), out_shape=...]
where the time goes in v5:
time: 66.9 us; the launch traced here: 66.8 us
  Pallas kernels  66.8 us (100%)
    pallas_call x1, Pallas kernels, per_device(): pl.pallas_call(functools.partial(relax_kernel, groups, slabs), out_shape=...  63.6 us
    pallas_call x1, Pallas kernels, per_device(): pl.pallas_call(scatter_kernel, out_shape=jax.ShapeDtypeStruct(orbitals.sh...  3.18 us

profile of v5, /device:TPU:2, one launch (start us, length us, event | category | flops | bytes accessed | tf_op | source)
XLA Modules:
  0.0 66.8 jit_solution(940917502797478220)
XLA Ops:
  0.0 63.6 %relax_pairs.1 = (f32[4,8,4,16,128]{4,3,2,1,0:T(8,128)S(1)}, f32[4,8,4,16,128]{4,3,2,1,0:T(8,128)S(1)}, s32[2,2,16]{2,1,0:T(2,128)S(1)}) custom-call(bf16[128,4,16,128]{3,2,1,0:T(8,128)(2,1)} %orb_hbm.1, f32[4,16,128]{2,1,0:T(8,128)} %diel_hbm.1, s32[1,2,2,16]{3,2,1,0:T(2,128)} %bitcast.1, s32[1,2]{1,0:T(1,128)} %count_hbm.1), custom_call_target="tpu_custom_call" | custom-call | tf_op jit(solution)/shard_map/relax_pairs/pallas_call | solution.py:497
  63.6 3.2 %add_by_row.1 = f32[128,4,16,128]{3,2,1,0:T(8,128)} custom-call(s32[1,2,2,16]{3,2,1,0:T(2,128)} %bitcast.2, s32[2,2,16]{2,1,0:T(2,128)S(1)} %get-tuple-element.8.asked, f32[4,8,4,16,128]{4,3,2,1,0:T(8,128)S(1)} %get-tuple-element.9.own, f32[4,8,4,16,128]{4,3,2,1,0:T(8,128)S(1)} %get-tuple-element.10.vis), custom_call_target="tpu_custom_call" | custom-call | tf_op jit(solution)/shard_map/add_by_row/pallas_call | solution.py:543

commit v6 on v5

--- a/solution.py
+++ b/solution.py
@@ -80,6 +80,8 @@
 
     far = (me // 2) % (groups // 4) == groups // 4 - 1
 
+    near = (me // 2) % (groups // 4) == 0
+
     def group(distance):
         return lax.rem(me + distance + groups, groups)
 
@@ -385,6 +387,12 @@
             def _():
                 give_back(batch).start()
 
+        elif batch == PUSHED:
+
+            @pl.when(jnp.logical_not(near))
+            def _():
+                give_back(batch).start()
+
         else:
             give_back(batch).start()
         for i in range(LANES):
@@ -426,6 +434,10 @@
     def _():
         for batch in range(PUSHED):
             give_back(batch).start()
+
+    @pl.when(near)
+    def _():
+        give_back(PUSHED).start()
 
     for step in range(STEPS):
         ask(step).wait_send()

time: 66.9 us -> 66.9 us (level)
  no operation moved by 1% of the time
where the time goes in v6:
time: 66.9 us; the launch traced here: 66.8 us
  Pallas kernels  66.8 us (100%)
    pallas_call x1, Pallas kernels, per_device(): pl.pallas_call(functools.partial(relax_kernel, groups, slabs), out_shape=...  63.6 us
    pallas_call x1, Pallas kernels, per_device(): pl.pallas_call(scatter_kernel, out_shape=jax.ShapeDtypeStruct(orbitals.sh...  3.18 us

profile of v6, /device:TPU:2, one launch (start us, length us, event | category | flops | bytes accessed | tf_op | source)
XLA Modules:
  0.0 66.8 jit_solution(13820237711212510956)
XLA Ops:
  0.0 63.6 %relax_pairs.1 = (f32[4,8,4,16,128]{4,3,2,1,0:T(8,128)S(1)}, f32[4,8,4,16,128]{4,3,2,1,0:T(8,128)S(1)}, s32[2,2,16]{2,1,0:T(2,128)S(1)}) custom-call(bf16[128,4,16,128]{3,2,1,0:T(8,128)(2,1)} %orb_hbm.1, f32[4,16,128]{2,1,0:T(8,128)} %diel_hbm.1, s32[1,2,2,16]{3,2,1,0:T(2,128)} %bitcast.1, s32[1,2]{1,0:T(1,128)} %count_hbm.1), custom_call_target="tpu_custom_call" | custom-call | tf_op jit(solution)/shard_map/relax_pairs/pallas_call | solution.py:509
  63.6 3.2 %add_by_row.1 = f32[128,4,16,128]{3,2,1,0:T(8,128)} custom-call(s32[1,2,2,16]{3,2,1,0:T(2,128)} %bitcast.2, s32[2,2,16]{2,1,0:T(2,128)S(1)} %get-tuple-element.8.asked, f32[4,8,4,16,128]{4,3,2,1,0:T(8,128)S(1)} %get-tuple-element.9.own, f32[4,8,4,16,128]{4,3,2,1,0:T(8,128)S(1)} %get-tuple-element.10.vis), custom_call_target="tpu_custom_call" | custom-call | tf_op jit(solution)/shard_map/add_by_row/pallas_call | solution.py:555
